TPU v7x, 32 devices: a whole 2x2x4 slice. The times are simulated.
32 devices in a mesh: dp: 8 (over y, x, core), tensor: 4 (over z).
Axes of the slice: x: 2, y: 2, z: 4, core: 2. Of those that a mesh axis runs over, the one named last changes fastest.
Arguments:
- residual: bfloat16 [4096, 4096], P(('dp', 'tensor')), may hold values from -3 to 3
- queries: bfloat16 [4096, 4096], P(('dp', 'tensor')), may hold values from -8 to 8
- rotated_key_states: bfloat16 [4096, 512], P(('dp', 'tensor')), may hold values from -8 to 8
- plain_value_states: bfloat16 [4096, 512], P(('dp', 'tensor')), may hold values from -24 to 24
- out_weight: bfloat16 [4096, 4096], P('tensor'), may hold values from -0.09375 to 0.09375
- norm_gain: bfloat16 [4096], replicated, may hold values from 0.099609375 to 1.8984375
- expert_ids: int32 [4096, 8], P(('dp', 'tensor')), may hold values from 0 to 31, all different within a row; in each aligned block of 128 rows (0 to 127, 128 to 255, ...) at most 36 rows name the same one
- gate_scales: float32 [4096, 8], P(('dp', 'tensor')), may hold values from 0.03 to 0.3
- w_gate: bfloat16 [32, 4096, 768], P(('dp', 'tensor')), may hold values from -0.09375 to 0.09375
- w_up: bfloat16 [32, 4096, 768], P(('dp', 'tensor')), may hold values from -0.09375 to 0.09375
- w_down: bfloat16 [32, 768, 4096], P(('dp', 'tensor')), may hold values from -0.21875 to 0.21875
Outputs:
- layer_out: bfloat16 [4096, 4096], P(('dp', 'tensor'))
Inputs may be any that keep to these rules, and one draw needn't show every extreme that they name: `expert_ids`: each row names 8 different experts; among the rows of one device (aligned blocks of 128 rows) no expert is named more than 36 times.
All inputs are finite; a program needn't handle non-finite values.
Results may differ from a plain program's by a relative error of at most 0.012.
Values may be sent and summed in bfloat16 or wider, within the bound.
No kernel may reach another device: no remote copies, remote signals or barrier semaphores. Data moves between devices by JAX's collectives and lax.ppermute only.
A program may use at most 192 MiB of HBM per device.

v0:
```python
import functools
import math

import jax
import jax.numpy as jnp
from jax import lax
from jax.experimental import pallas as pl
from jax.experimental.pallas import tpu as pltpu
from jax.sharding import PartitionSpec as P

D = 4096
QUERY_HEADS = 32
KEY_VALUE_HEADS = 4
HEAD_SIZE = 128
TOPK = 8


def attend_kernel(
    q_ref, k_ref, v_ref, weight_ref, o_ref, attended_ref, held_ref, sem, *, block, attend_steps
):
    step = pl.program_id(0)
    scaling = 1.0 / math.sqrt(HEAD_SIZE)
    total, lanes = q_ref.shape
    heads = lanes // HEAD_SIZE
    fetch = pltpu.make_async_copy(weight_ref, held_ref, sem)

    @pl.when(step == 0)
    def _():
        fetch.start()

    @pl.when(step < attend_steps)
    def _():
        rows = lax.broadcasted_iota(jnp.int32, (block, block), 0)
        cols = lax.broadcasted_iota(jnp.int32, (block, block), 1)
        for first in range(0, total, block):
            seen = first + block
            mixes = []
            for head in range(heads):
                scores = (
                    lax.dot_general(
                        q_ref[first:seen, head * HEAD_SIZE : (head + 1) * HEAD_SIZE],
                        k_ref[:seen, :],
                        (((1,), (1,)), ((), ())),
                        preferred_element_type=jnp.float32,
                    )
                    * scaling
                )
                diagonal = jnp.where(cols <= rows, scores[:, first:], -1e30)
                if first:
                    scores = jnp.concatenate([scores[:, :first], diagonal], axis=1)
                else:
                    scores = diagonal
                peak = jnp.max(scores, axis=-1, keepdims=True)
                expons = jnp.exp(scores - peak)
                totals = jnp.sum(expons, axis=-1, keepdims=True)
                mixed = jnp.dot(
                    expons.astype(jnp.bfloat16), v_ref[:seen, :], preferred_element_type=jnp.float32
                )
                mixes.append((mixed / totals).astype(jnp.bfloat16))
            start = pl.multiple_of(step * lanes, lanes)
            attended_ref[first:seen, pl.ds(start, lanes)] = jnp.concatenate(mixes, axis=1)

    @pl.when(step == attend_steps)
    def _():
        fetch.wait()

    @pl.when(step >= attend_steps)
    def _():
        tile = o_ref.shape[1]
        start = pl.multiple_of((step - attend_steps) * tile, tile)
        o_ref[...] = jnp.dot(
            attended_ref[...], held_ref[:, pl.ds(start, tile)], preferred_element_type=jnp.float32
        ).astype(jnp.bfloat16)


def attend_and_project(slab, out_weight, heads, tile=512):
    positions = slab.shape[0]
    width = out_weight.shape[1]
    out_weight = pltpu.with_memory_space_constraint(out_weight, pltpu.HBM)
    group = 2 if heads % 2 == 0 else 1
    attend_steps = heads // group
    last = attend_steps - 1
    return pl.pallas_call(
        functools.partial(attend_kernel, block=128, attend_steps=attend_steps),
        grid=(attend_steps + width // tile,),
        in_specs=[
            pl.BlockSpec((positions, group * HEAD_SIZE), lambda i: (0, jnp.minimum(i, last))),
            pl.BlockSpec((positions, HEAD_SIZE), lambda i: (0, heads)),
            pl.BlockSpec((positions, HEAD_SIZE), lambda i: (0, heads + 1)),
            pl.BlockSpec(memory_space=pl.ANY),
        ],
        out_specs=pl.BlockSpec((positions, tile), lambda i: (0, jnp.maximum(i - attend_steps, 0))),
        out_shape=pltpu.HBM((positions, width), jnp.bfloat16),
        scratch_shapes=[
            pltpu.VMEM((positions, heads * HEAD_SIZE), jnp.bfloat16),
            pltpu.VMEM(out_weight.shape, jnp.bfloat16),
            pltpu.SemaphoreType.DMA,
        ],
        compiler_params=pltpu.CompilerParams(vmem_limit_bytes=40 * 1024 * 1024),
    )(slab, slab, slab, out_weight)


def slot_plan(capacity):
    whole = capacity // 8 * 8
    if capacity - whole > 4:
        whole += 8
    return whole, max(capacity - whole, 0)


def per_source(refs, sources, stride):
    if len(refs) == 1:
        return [(refs[0], source * stride) for source in range(sources)]
    return [(ref, 0) for ref in refs]


def expert_kernel(*refs, arrays_in, arrays_out, sources, whole, rest, tile):
    rows_refs, refs = refs[:arrays_in], refs[arrays_in:]
    gate_ref, up_ref, down_ref = refs[:3]
    out_refs, refs = refs[3 : 3 + arrays_out], refs[3 + arrays_out :]
    full_ref, act_ref, gates, ups, downs, sems = refs
    width, units = gate_ref.shape
    half = width // 2
    tiles = units // tile
    pieces = []
    for index in range(tiles):
        window = slice(index * tile, (index + 1) * tile)
        pieces.append((gate_ref.at[:, window], gates.at[index]))
        pieces.append((up_ref.at[:, window], ups.at[index]))
    for side in range(2):
        pieces.append((down_ref.at[:, side * half : (side + 1) * half], downs.at[side]))
    copies = [
        pltpu.make_async_copy(source, target, sems.at[index])
        for index, (source, target) in enumerate(pieces)
    ]
    for copy in copies:
        copy.start()
    stride = 2 * whole + (8 if rest else 0)
    count = sources * whole
    taken = per_source(rows_refs, sources, stride)
    for source, (ref, base) in enumerate(taken):
        for side in range(2):
            first = base + side * whole
            full_ref[source * whole : (source + 1) * whole, side * half : (side + 1) * half] = ref[
                first : first + whole, :
            ]
    if rest:
        last = [ref[base + 2 * whole : base + stride, :].astype(jnp.float32) for ref, base in taken]
        last = jnp.concatenate(last, axis=0)
        full_ref[count:, :half] = last.astype(jnp.bfloat16)
        full_ref[count:, half:] = pltpu.roll(last, last.shape[0] - 4, 0).astype(jnp.bfloat16)
    def gated(index, carry):
        window = pl.ds(pl.multiple_of(index * tile, tile), tile)
        pltpu.make_async_copy(gate_ref.at[:, window], gates.at[index], sems.at[2 * index]).wait()
        gate_part = jnp.dot(full_ref[...], gates[index], preferred_element_type=jnp.float32)
        pltpu.make_async_copy(up_ref.at[:, window], ups.at[index], sems.at[2 * index + 1]).wait()
        up_part = jnp.dot(full_ref[...], ups[index], preferred_element_type=jnp.float32)
        act_ref[:, window] = (gate_part / (1.0 + jnp.exp(-gate_part)) * up_part).astype(jnp.bfloat16)
        return carry

    lax.fori_loop(0, tiles, gated, 0)
    copies[2 * tiles].wait()
    copies[2 * tiles + 1].wait()
    given = per_source(out_refs, sources, stride)
    spread = 512

    def lower(index, carry):
        window = pl.ds(pl.multiple_of(index * spread, spread), spread)
        kept = None
        for side in range(2):
            produced = jnp.dot(
                act_ref[...], downs[side, :, window], preferred_element_type=jnp.float32
            )
            rounded = produced[:count].astype(jnp.bfloat16)
            for source, (ref, base) in enumerate(given):
                top = base + side * whole
                ref[top : top + whole, window] = rounded[source * whole : (source + 1) * whole]
            if rest and side == 0:
                kept = produced[count:]
            elif rest:
                moved = pltpu.roll(produced[count:], 4, 0)
                low = lax.broadcasted_iota(jnp.int32, kept.shape, 0) % 8 < 4
                merged = jnp.where(low, kept, moved).astype(jnp.bfloat16)
                for source, (ref, base) in enumerate(given):
                    ref[base + 2 * whole : base + stride, window] = merged[source * 8 : (source + 1) * 8]
        return carry

    lax.fori_loop(0, half // spread, lower, 0)


def run_expert(arrived, weights, sources, whole, rest, arrays_out, tile=256):
    width, units = weights[0].shape
    padded = sources * (whole + (8 if rest else 0))
    stride = 2 * whole + (8 if rest else 0)
    out_shape = jax.ShapeDtypeStruct((sources * stride // arrays_out, width // 2), jnp.bfloat16)
    inside = pl.BlockSpec(memory_space=pltpu.VMEM)
    return pl.pallas_call(
        functools.partial(
            expert_kernel,
            arrays_in=len(arrived),
            arrays_out=arrays_out,
            sources=sources,
            whole=whole,
            rest=rest,
            tile=tile,
        ),
        in_specs=[inside] * len(arrived) + [pl.BlockSpec(memory_space=pl.ANY)] * 3,
        out_specs=[inside] * arrays_out,
        out_shape=[out_shape] * arrays_out,
        scratch_shapes=[
            pltpu.VMEM((padded, width), jnp.bfloat16),
            pltpu.VMEM((padded, units), jnp.bfloat16),
            pltpu.VMEM((units // tile, width, tile), jnp.bfloat16),
            pltpu.VMEM((units // tile, width, tile), jnp.bfloat16),
            pltpu.VMEM((2, units, width // 2), jnp.bfloat16),
            pltpu.SemaphoreType.DMA((2 * (units // tile) + 2,)),
        ],
        compiler_params=pltpu.CompilerParams(vmem_limit_bytes=48 * 1024 * 1024),
        cost_estimate=pl.CostEstimate(
            flops=6 * padded * width * units, transcendentals=padded * units, bytes_accessed=40_000_000
        ),
    )(*arrived, *weights)


def gather_kernel(pick_ref, *refs, block_count):
    block_refs, out_refs = refs[:block_count], refs[block_count:]
    step = pick_ref.shape[0] // len(out_refs)
    spread = 512

    def part(place, carry):
        window = pl.ds(pl.multiple_of(place * spread, spread), spread)
        block = block_refs[0][:, window]
        for ref in block_refs[1:]:
            block = block + ref[:, window]
        for index, ref in enumerate(out_refs):
            ref[:, window] = jnp.dot(
                pick_ref[index * step : (index + 1) * step, :],
                block,
                preferred_element_type=jnp.float32,
            ).astype(jnp.bfloat16)
        return carry

    lax.fori_loop(0, block_refs[0].shape[1] // spread, part, 0)


def gather_rows(pick, blocks, arrays_out):
    out_shape = jax.ShapeDtypeStruct((pick.shape[0] // arrays_out, blocks[0].shape[1]), jnp.bfloat16)
    inside = pl.BlockSpec(memory_space=pltpu.VMEM)
    return pl.pallas_call(
        functools.partial(gather_kernel, block_count=len(blocks)),
        in_specs=[inside] * (1 + len(blocks)),
        out_specs=[inside] * arrays_out,
        out_shape=[out_shape] * arrays_out,
        cost_estimate=pl.CostEstimate(
            flops=2 * pick.size * blocks[0].shape[1], transcendentals=0, bytes_accessed=4_000_000
        ),
    )(pick, *blocks)


def combine_kernel(blend_ref, rows_ref, *out_refs):
    rows = out_refs[0].shape[0]
    spread = 512

    def part(place, carry):
        window = pl.ds(pl.multiple_of(place * spread, spread), spread)
        for index, ref in enumerate(out_refs):
            ref[:, window] = jnp.dot(
                blend_ref[index * rows : (index + 1) * rows, :],
                rows_ref[:, window],
                preferred_element_type=jnp.float32,
            ).astype(ref.dtype)
        return carry

    lax.fori_loop(0, rows_ref.shape[1] // spread, part, 0)


def combine_rows(blend, returned, kind, arrays_out=1):
    out_shape = jax.ShapeDtypeStruct((blend.shape[0] // arrays_out, returned.shape[1]), kind)
    inside = pl.BlockSpec(memory_space=pltpu.VMEM)
    return pl.pallas_call(
        combine_kernel,
        in_specs=[inside] * 2,
        out_specs=[inside] * arrays_out,
        out_shape=[out_shape] * arrays_out,
        cost_estimate=pl.CostEstimate(
            flops=2 * blend.size * out_shape.shape[1], transcendentals=0, bytes_accessed=4_000_000
        ),
    )(blend, returned)


def swap(value, axis, distance, size):
    return lax.ppermute(value, axis, [(i, i ^ distance) for i in range(size)])


def exchange(rows, size):
    if len(rows) > 1:
        return [swap(part, "dp", k, size) if k else part for k, part in enumerate(rows)]
    (rows,) = rows
    parted = rows.reshape(size, rows.shape[0] // size, rows.shape[1])
    parted = lax.all_to_all(parted, "dp", split_axis=0, concat_axis=0, tiled=True)
    return [parted.reshape(rows.shape)]


def after(*values):
    return lax.optimization_barrier(values)


def selection(ids, gates, experts, whole, rest):
    match = (ids[:, :, None] == experts[None, None, :]).astype(jnp.float32)
    chosen = jnp.sum(match, axis=1)
    weight = jnp.sum(match * gates[:, :, None], axis=1)
    rows = ids.shape[0]
    order = jnp.arange(rows, dtype=jnp.int32)
    earlier = (order[:, None] > order[None, :]).astype(jnp.bfloat16)
    ranks = jnp.dot(earlier, chosen.astype(jnp.bfloat16), preferred_element_type=jnp.float32)
    slot_of = jnp.where(chosen > 0, ranks.astype(jnp.int32), -1)
    stride = 2 * whole + (8 if rest else 0)
    column = jnp.arange(experts.shape[0] * stride, dtype=jnp.int32)
    owner, inner = column // stride, column % stride
    ending = inner - 2 * whole
    side = jnp.where(ending < 0, inner // max(whole, 1), ending // 4)
    place = jnp.where(ending < 0, inner % max(whole, 1), whole + ending % 4)
    place = jnp.where(place < whole + rest, place, -2)
    count = column.shape[0]
    expand = owner[None, :] == jnp.arange(experts.shape[0], dtype=jnp.int32)[:, None]
    wide_slot = jnp.sum(jnp.where(expand[None], slot_of[:, :, None], 0), axis=1)
    wide_weight = jnp.sum(jnp.where(expand[None], weight[:, :, None], 0.0), axis=1)
    sides = jnp.arange(2, dtype=jnp.int32)
    hit = (wide_slot == place[None, :])[None] & (side[None, None, :] == sides[:, None, None])
    blend = jnp.where(hit, wide_weight[None], 0.0).reshape(2 * rows, count).astype(jnp.bfloat16)
    pick = hit.reshape(2 * rows, count).astype(jnp.bfloat16).T
    return pick, blend


def per_device(
    residual,
    queries,
    rotated_key_states,
    plain_value_states,
    out_weight,
    norm_gain,
    expert_ids,
    gate_scales,
    w_gate,
    w_up,
    w_down,
):
    row_count = residual.shape[0]
    tensor_size = lax.axis_size("tensor")
    dp_size = lax.axis_size("dp")
    my_tensor = lax.axis_index("tensor")
    my_dp = lax.axis_index("dp")
    heads = QUERY_HEADS // tensor_size
    shares = tensor_size // KEY_VALUE_HEADS

    routing = jnp.concatenate([expert_ids.astype(jnp.float32), gate_scales], axis=1)

    def by_head(states):
        states = states.reshape(row_count, KEY_VALUE_HEADS, HEAD_SIZE)
        return jnp.repeat(states, shares, axis=1) if shares > 1 else states

    slabs = jnp.concatenate(
        [
            queries.reshape(row_count, tensor_size, heads * HEAD_SIZE),
            by_head(rotated_key_states),
            by_head(plain_value_states),
        ],
        axis=2,
    )
    slab = lax.all_to_all(slabs, "tensor", split_axis=1, concat_axis=0, tiled=True)
    slab = slab.reshape(tensor_size * row_count, (heads + 2) * HEAD_SIZE)
    projected = lax.psum_scatter(
        attend_and_project(slab, out_weight, heads),
        "tensor",
        scatter_dimension=0,
        tiled=True,
    ).astype(jnp.float32)
    hidden_state = residual.astype(jnp.float32) + projected
    inverse_rms = lax.rsqrt(jnp.mean(hidden_state * hidden_state, axis=-1, keepdims=True) + 1e-06)
    normed = (hidden_state * inverse_rms * norm_gain.astype(jnp.float32)).astype(jnp.bfloat16)
    normed = jnp.concatenate([normed[:, : D // 2], normed[:, D // 2 :]], axis=0)

    capacity = 9 * row_count // (dp_size * tensor_size)
    peers = jnp.arange(dp_size, dtype=jnp.int32)
    whole, rest = slot_plan(capacity)

    weights = (w_gate[0], w_up[0], w_down[0])

    def plan_for(routing, arrays):
        owners = peers if arrays == 1 else my_dp ^ peers
        return selection(
            routing[:, :TOPK].astype(jnp.int32),
            routing[:, TOPK:],
            owners * tensor_size + my_tensor,
            whole,
            rest,
        )

    def expert(arrived):
        return run_expert(arrived, weights, dp_size, whole, rest, len(arrived))

    def short(value):
        return value.astype(jnp.bfloat16)

    def long(value):
        return value.astype(jnp.float32)

    if tensor_size == 4:
        pairs = [(0, 1), (1, 0), (2, 3), (3, 2)]
        middle = [(1, 2), (2, 1)]
        outward = [(1, 0), (2, 3)]
        inward = [(0, 1), (3, 2)]
        ends = [(0, 3), (3, 0)]
        skips = [(1, 3), (2, 0)]

        def send(value, moves):
            return lax.ppermute(value, "tensor", moves)

        def spread(block):
            near = send(block, pairs)
            inner_two = send(block, middle)
            outer_two = send(inner_two, outward)
            inner_three = send(near, middle)
            outer_three = send(inner_three, outward)
            return near, inner_two, outer_two, inner_three, outer_three

        r_near, r_in2, r_out2, r_in3, r_out3 = spread(routing)
        arrays = (1, 1, 1, 1)
        plans = [
            plan_for(r, n)
            for r, n in zip((routing, r_near, r_in2 + r_out2, r_in3 + r_out3), arrays)
        ]

        normed, *flat = after(normed, *[part for plan in plans for part in plan])
        plans = list(zip(flat[::2], flat[1::2]))

        def dispatch(blocks, chunk):
            return gather_rows(plans[chunk][0], blocks, arrays[chunk])

        def combine(returned, chunk, kind=jnp.bfloat16, arrays_out=1):
            return list(combine_rows(plans[chunk][1], returned[0], kind, arrays_out))

        near = send(normed, pairs)
        inner_two = send(normed, middle)
        out0 = dispatch([normed], 0)
        arr0 = exchange(out0, dp_size)
        near, inner_two, _ = after(near, inner_two, out0)
        outer_two = send(inner_two, outward)
        inner_three = send(near, middle)
        out1 = dispatch([near], 1)
        arr1 = exchange(out1, dp_size)
        arr0, _ = after(arr0, out1)
        pro0 = expert(arr0)
        outer_two, inner_three, _ = after(outer_two, inner_three, pro0)
        outer_three = send(inner_three, outward)
        out2 = dispatch([inner_two, outer_two], 2)
        arr2 = exchange(out2, dp_size)
        arr1, _ = after(arr1, out2)
        pro1 = expert(arr1)
        outer_three, _ = after(outer_three, pro1)
        out3 = dispatch([inner_three, outer_three], 3)
        arr3 = exchange(out3, dp_size)
        arr2, pro1, _ = after(arr2, pro1, out3)
        pro2 = expert(arr2)
        arr3, pro2 = after(arr3, pro2)
        ret2 = exchange(pro2, dp_size)
        pro3 = expert(arr3)
        ret2, pro3 = after(ret2, pro3)
        ret3 = exchange(pro3, dp_size)
        part2 = combine(ret2, 2, arrays_out=2)
        far2 = [send(part2[side], inward) for side in range(2)]
        pro1, ret3, far2[0], far2[1] = after(pro1, ret3, *far2)
        ret1 = exchange(pro1, dp_size)
        part3 = combine(ret3, 3, arrays_out=2)
        far3 = [send(part3[side], inward) for side in range(2)]
        part2[0], part2[1], _ = after(*part2, part3[0])
        last2 = [send(short(long(part2[side]) + long(far2[side])), middle) for side in range(2)]
        pro0, ret1, far3[0], far3[1], last2[0], last2[1] = after(pro0, ret1, *far3, *last2)
        ret0 = exchange(pro0, dp_size)
        mid3 = [send(short(long(part3[0]) + long(far3[0])), middle), None]
        mid3[0], far3[1] = after(mid3[0], far3[1])
        mid3[1] = send(short(long(part3[1]) + long(far3[1])), middle)
        part1 = combine(ret1, 1, jnp.float32, arrays_out=2)
        last1 = [send(short(part1[side] + long(mid3[side])), pairs) for side in range(2)]
        home = combine(ret0, 0, jnp.float32, arrays_out=2)
        moe_sum = jnp.concatenate(
            [home[side] + long(last1[side]) + long(last2[side]) for side in range(2)], axis=0
        )
    else:
        blocks = {0: normed}
        moe_sum = 0.0
        for step in range(tensor_size):
            if step:
                low = step & -step
                blocks[step] = swap(blocks[step ^ low], "tensor", low, tensor_size)
            plan = plan_for(swap(routing, "tensor", step, tensor_size) if step else routing, 1)
            arrived = exchange(gather_rows(plan[0], [blocks[step]], 1), dp_size)
            (blended,) = combine_rows(plan[1], exchange(expert(arrived), dp_size)[0], jnp.float32)
            if step:
                blended = long(swap(short(blended), "tensor", step, tensor_size))
            moe_sum = moe_sum + blended
    moe_sum = jnp.concatenate([moe_sum[:row_count], moe_sum[row_count:]], axis=1)
    return (hidden_state + moe_sum).astype(jnp.bfloat16)


def solution(mesh):
    placed = (
        P(("dp", "tensor"), None),
        P(("dp", "tensor"), None),
        P(("dp", "tensor"), None),
        P(("dp", "tensor"), None),
        P("tensor", None),
        P(),
        P(("dp", "tensor"), None),
        P(("dp", "tensor"), None),
        P(("dp", "tensor"), None, None),
        P(("dp", "tensor"), None, None),
        P(("dp", "tensor"), None, None),
    )
    return jax.shard_map(
        per_device, mesh=mesh, in_specs=placed, out_specs=P(("dp", "tensor"), None), check_vma=False
    )
```

profile of v0, /device:TPU:10, one launch (start us, length us, event | category | flops | bytes accessed | tf_op | source)
XLA Modules:
  0.0 459.5 jit_solution(8672874553635883257)
XLA Ops:
  9.0 34.7 %all_to_all.55 = bf16[128,4,1280]{2,0,1:T(8,128)(2,1)S(1)} all-to-all(bf16[128,4,1280]{2,0,1:T(8,128)(2,1)S(1)} %pad_maximum_fusion), channel_id=1, replica_groups=mesh['dp'=8,'tensor'=4] {'tensor'}, dimensions={1} | all-to-all | bytes 2621440 | tf_op jit(solution)/shard_map/all_to_all | solution.py:369
  43.6 15.9 %shard_map.109 = bf16[512,4096]{1,0:T(8,128)(2,1)} custom-call(bf16[512,1280]{1,0:T(8,128)(2,1)S(1)} %bitcast.50, bf16[512,1280]{1,0:T(8,128)(2,1)S(1)} %bitcast.51, bf16[512,1280]{1,0:T(8,128)(2,1)S(1)} %bitcast.52, bf16[1024,4096]{1,0:T(8,128)(2,1)} %weight_ref.1), custom_call_target="tpu_custom_call" | custom-call | tf_op jit(solution)/shard_map/pallas_call | solution.py:83
  84.8 52.2 %reduce-scatter.2.cloned.1.call-done = bf16[128,4096]{1,0:T(8,128)(2,1)} async-done(((bf16[512,4096]{1,0:T(8,128)(2,1)}), bf16[128,4096]{1,0:T(8,128)(2,1)}) %reduce-scatter.2.cloned.1.call-update) | async-done | bytes 1048592 | tf_op jit(solution)/shard_map/reduce_scatter | solution.py:371
  152.8 21.3 %collective-permute-done.5.refs_0_ = bf16[256,2048]{1,0:T(8,128)(2,1)} collective-permute-done((bf16[256,2048]{1,0:T(8,128)(2,1)}, bf16[256,2048]{1,0:T(8,128)(2,1)}, u32[]{:S(2)}, u32[]{:S(2)}) %collective-permute-start.5) | collective-permute-done | bytes 1048608 | tf_op jit(solution)/shard_map/ppermute | solution.py:416
  180.5 4.6 %all-to-all-start.3 = ((bf16[8,72,2048]{2,1,0:T(8,128)(2,1)}), bf16[8,72,2048]{2,1,0:T(8,128)(2,1)}, u32[]{:S(2)}, u32[]{:S(2)}) async-start(bf16[8,72,2048]{2,1,0:T(8,128)(2,1)} %bitcast.68), calls=%async_computation.4 | async-start | bytes 4718592 | tf_op jit(solution)/shard_map/all_to_all | solution.py:299
  190.8 14.9 %shard_map.112 = bf16[576,2048]{1,0:T(8,128)(2,1)} custom-call(bf16[576,2048]{1,0:T(8,128)(2,1)S(1)} %bitcast.53, bf16[4096,768]{1,0:T(8,128)(2,1)} %bitcast.56, bf16[4096,768]{1,0:T(8,128)(2,1)} %bitcast.60, bf16[768,4096]{1,0:T(8,128)(2,1)} %bitcast.64), custom_call_target="tpu_custom_call" | custom-call | flops 6039797760 | bytes 40000000 | tf_op jit(solution)/shard_map/pallas_call | solution.py:196
  209.7 5.1 %collective-permute-done.8.refs_0_ = bf16[256,2048]{1,0:T(8,128)(2,1)} collective-permute-done((bf16[256,2048]{1,0:T(8,128)(2,1)}, bf16[256,2048]{1,0:T(8,128)(2,1)}, u32[]{:S(2)}, u32[]{:S(2)}) %collective-permute-start.8) | collective-permute-done | bytes 1048608 | tf_op jit(solution)/shard_map/ppermute | solution.py:416
  225.7 16.5 %shard_map.114 = bf16[576,2048]{1,0:T(8,128)(2,1)} custom-call(bf16[576,2048]{1,0:T(8,128)(2,1)} %bitcast.23.refs_0_, bf16[4096,768]{1,0:T(8,128)(2,1)} %bitcast.57, bf16[4096,768]{1,0:T(8,128)(2,1)} %bitcast.61, bf16[768,4096]{1,0:T(8,128)(2,1)} %bitcast.65), custom_call_target="tpu_custom_call" | custom-call | flops 6039797760 | bytes 40000000 | tf_op jit(solution)/shard_map/pallas_call | solution.py:196
  242.2 5.8 %collective-permute-done.9.refs_1_ = bf16[256,2048]{1,0:T(8,128)(2,1)} collective-permute-done((bf16[256,2048]{1,0:T(8,128)(2,1)}, bf16[256,2048]{1,0:T(8,128)(2,1)}, u32[]{:S(2)}, u32[]{:S(2)}) %collective-permute-start.9) | collective-permute-done | bytes 1048608 | tf_op jit(solution)/shard_map/ppermute | solution.py:416
  252.3 4.8 %all-to-all-start.4 = ((bf16[8,72,2048]{2,1,0:T(8,128)(2,1)}), bf16[8,72,2048]{2,1,0:T(8,128)(2,1)}, u32[]{:S(2)}, u32[]{:S(2)}) async-start(bf16[8,72,2048]{2,1,0:T(8,128)(2,1)} %bitcast.74), calls=%async_computation.5 | async-start | bytes 4718592 | tf_op jit(solution)/shard_map/all_to_all | solution.py:299
  257.1 13.4 %shard_map.116 = bf16[576,2048]{1,0:T(8,128)(2,1)S(1)} custom-call(bf16[576,2048]{1,0:T(8,128)(2,1)S(1)} %bitcast.54, bf16[4096,768]{1,0:T(8,128)(2,1)} %bitcast.58, bf16[4096,768]{1,0:T(8,128)(2,1)} %bitcast.62, bf16[768,4096]{1,0:T(8,128)(2,1)} %bitcast.66), custom_call_target="tpu_custom_call" | custom-call | flops 6039797760 | bytes 40000000 | tf_op jit(solution)/shard_map/pallas_call | solution.py:196
  271.9 13.2 %all-to-all-done.4 = bf16[8,72,2048]{2,1,0:T(8,128)(2,1)} async-done(((bf16[8,72,2048]{2,1,0:T(8,128)(2,1)}), bf16[8,72,2048]{2,1,0:T(8,128)(2,1)}, u32[]{:S(2)}, u32[]{:S(2)}) %all-to-all-start.4) | async-done | bytes 2359328 | tf_op jit(solution)/shard_map/all_to_all | solution.py:299
  285.2 5.0 %all-to-all-start.5 = ((bf16[8,72,2048]{2,1,0:T(8,128)(2,1)}), bf16[8,72,2048]{2,1,0:T(8,128)(2,1)S(1)}, u32[]{:S(2)}, u32[]{:S(2)}) async-start(bf16[8,72,2048]{2,1,0:T(8,128)(2,1)} %bitcast.55), calls=%async_computation.6 | async-start | bytes 4718592 | tf_op jit(solution)/shard_map/all_to_all | solution.py:299
  290.2 16.5 %shard_map.117 = bf16[576,2048]{1,0:T(8,128)(2,1)} custom-call(bf16[576,2048]{1,0:T(8,128)(2,1)} %bitcast.25.refs_0_, bf16[4096,768]{1,0:T(8,128)(2,1)} %bitcast.59, bf16[4096,768]{1,0:T(8,128)(2,1)} %bitcast.63, bf16[768,4096]{1,0:T(8,128)(2,1)} %bitcast.67), custom_call_target="tpu_custom_call" | custom-call | flops 6039797760 | bytes 40000000 | tf_op jit(solution)/shard_map/pallas_call | solution.py:196
  306.7 11.4 %all-to-all-done.5 = bf16[8,72,2048]{2,1,0:T(8,128)(2,1)S(1)} async-done(((bf16[8,72,2048]{2,1,0:T(8,128)(2,1)}), bf16[8,72,2048]{2,1,0:T(8,128)(2,1)S(1)}, u32[]{:S(2)}, u32[]{:S(2)}) %all-to-all-start.5) | async-done | bytes 2359328 | tf_op jit(solution)/shard_map/all_to_all | solution.py:299
  319.6 5.0 %all-to-all-start.6 = ((bf16[8,72,2048]{2,1,0:T(8,128)(2,1)}), bf16[8,72,2048]{2,1,0:T(8,128)(2,1)S(1)}, u32[]{:S(2)}, u32[]{:S(2)}) async-start(bf16[8,72,2048]{2,1,0:T(8,128)(2,1)} %bitcast.28), calls=%async_computation.7 | async-start | bytes 4718592 | tf_op jit(solution)/shard_map/all_to_all | solution.py:299
  331.4 14.3 %collective-permute-done.10 = bf16[128,2048]{1,0:T(8,128)(2,1)S(1)} collective-permute-done((bf16[128,2048]{1,0:T(8,128)(2,1)}, bf16[128,2048]{1,0:T(8,128)(2,1)S(1)}, u32[]{:S(2)}, u32[]{:S(2)}) %collective-permute-start.10) | collective-permute-done | bytes 524320 | tf_op jit(solution)/shard_map/ppermute | solution.py:416
  346.5 9.7 %collective-permute-done.11 = bf16[128,2048]{1,0:T(8,128)(2,1)} collective-permute-done((bf16[128,2048]{1,0:T(8,128)(2,1)}, bf16[128,2048]{1,0:T(8,128)(2,1)}, u32[]{:S(2)}, u32[]{:S(2)}) %collective-permute-start.11) | collective-permute-done | bytes 524320 | tf_op jit(solution)/shard_map/ppermute | solution.py:416
  377.3 8.2 %collective-permute-done.15 = bf16[128,2048]{1,0:T(8,128)(2,1)S(1)} collective-permute-done((bf16[128,2048]{1,0:T(8,128)(2,1)S(1)}, bf16[128,2048]{1,0:T(8,128)(2,1)S(1)}, u32[]{:S(2)}, u32[]{:S(2)}) %collective-permute-start.15) | collective-permute-done | bytes 524320 | tf_op jit(solution)/shard_map/ppermute | solution.py:416
  385.5 10.4 %collective-permute-done.14 = bf16[128,2048]{1,0:T(8,128)(2,1)S(1)} collective-permute-done((bf16[128,2048]{1,0:T(8,128)(2,1)S(1)}, bf16[128,2048]{1,0:T(8,128)(2,1)S(1)}, u32[]{:S(2)}, u32[]{:S(2)}) %collective-permute-start.14) | collective-permute-done | bytes 524320 | tf_op jit(solution)/shard_map/ppermute | solution.py:416
  403.9 4.6 %all-to-all-start.8 = ((bf16[8,72,2048]{2,1,0:T(8,128)(2,1)}), bf16[8,72,2048]{2,1,0:T(8,128)(2,1)}, u32[]{:S(2)}, u32[]{:S(2)}) async-start(bf16[8,72,2048]{2,1,0:T(8,128)(2,1)} %bitcast.32), calls=%async_computation.9 | async-start | bytes 4718592 | tf_op jit(solution)/shard_map/all_to_all | solution.py:299
  408.6 7.2 %collective-permute-done.16 = bf16[128,2048]{1,0:T(8,128)(2,1)} collective-permute-done((bf16[128,2048]{1,0:T(8,128)(2,1)}, bf16[128,2048]{1,0:T(8,128)(2,1)}, u32[]{:S(2)}, u32[]{:S(2)}) %collective-permute-start.16) | collective-permute-done | bytes 524320 | tf_op jit(solution)/shard_map/ppermute | solution.py:416
  436.7 4.6 shard_map.120
  443.1 7.0 %collective-permute-done.19 = bf16[128,2048]{1,0:T(8,128)(2,1)} collective-permute-done((bf16[128,2048]{1,0:T(8,128)(2,1)}, bf16[128,2048]{1,0:T(8,128)(2,1)}, u32[]{:S(2)}, u32[]{:S(2)}) %collective-permute-start.19) | collective-permute-done | bytes 524320 | tf_op jit(solution)/shard_map/ppermute | solution.py:416
  (146 shorter events, 139.2 us)
Async XLA Ops:
  6.5 130.4 %reduce-scatter.2.cloned.1.call-start = ((), (), s32[]{:S(2)}) async-start(), calls=%async_computation.10 | async-start | bytes 5242880 | tf_op jit(solution)/shard_map/reduce_scatter | solution.py:371
  144.3 36.2 %all-to-all-start.1 = ((bf16[8,72,2048]{2,1,0:T(8,128)(2,1)}), bf16[8,72,2048]{2,1,0:T(8,128)(2,1)S(1)}, u32[]{:S(2)}, u32[]{:S(2)}) async-start(bf16[8,72,2048]{2,1,0:T(8,128)(2,1)} %bitcast.69), calls=%async_computation.2 | async-start | bytes 4718592 | tf_op jit(solution)/shard_map/all_to_all | solution.py:299
  148.6 25.5 %collective-permute-start.5 = (bf16[256,2048]{1,0:T(8,128)(2,1)}, bf16[256,2048]{1,0:T(8,128)(2,1)}, u32[]{:S(2)}, u32[]{:S(2)}) collective-permute-start(bf16[256,2048]{1,0:T(8,128)(2,1)} %pad_maximum_fusion.1.refs_0_), channel_id=1, source_target_pairs={{0,1},{1,0},{2,3},{3,2},{4,5},{5,4},{6,7},{7,6},{8,9},{9,8},{10,11... | collective-permute-start | bytes 3145736 | tf_op jit(solution)/shard_map/ppermute | solution.py:416
  149.4 27.1 %collective-permute-start.6 = (bf16[256,2048]{1,0:T(8,128)(2,1)}, bf16[256,2048]{1,0:T(8,128)(2,1)}, u32[]{:S(2)}, u32[]{:S(2)}) collective-permute-start(bf16[256,2048]{1,0:T(8,128)(2,1)} %pad_maximum_fusion.1.refs_0_), channel_id=1, source_target_pairs={{1,2},{2,1},{5,6},{6,5},{9,10},{10,9},{13,14},{14,13},{17,18},{18,... | collective-permute-start | bytes 3145736 | tf_op jit(solution)/shard_map/ppermute | solution.py:416
  180.5 38.7 %all-to-all-start.3 = ((bf16[8,72,2048]{2,1,0:T(8,128)(2,1)}), bf16[8,72,2048]{2,1,0:T(8,128)(2,1)}, u32[]{:S(2)}, u32[]{:S(2)}) async-start(bf16[8,72,2048]{2,1,0:T(8,128)(2,1)} %bitcast.68), calls=%async_computation.4 | async-start | bytes 4718592 | tf_op jit(solution)/shard_map/all_to_all | solution.py:299
  185.1 24.6 %collective-permute-start.7 = (bf16[256,2048]{1,0:T(8,128)(2,1)}, bf16[256,2048]{1,0:T(8,128)(2,1)}, u32[]{:S(2)}, u32[]{:S(2)}) collective-permute-start(bf16[256,2048]{1,0:T(8,128)(2,1)} %collective-permute-done.6.refs_0_), channel_id=1, source_target_pairs={{1,0},{2,3},{5,4},{6,7},{9,8},{10,11},{13,12},{14,15},{17,16},{18,... | collective-permute-start | bytes 3145736 | tf_op jit(solution)/shard_map/ppermute | solution.py:416
  187.4 27.4 %collective-permute-start.8 = (bf16[256,2048]{1,0:T(8,128)(2,1)}, bf16[256,2048]{1,0:T(8,128)(2,1)}, u32[]{:S(2)}, u32[]{:S(2)}) collective-permute-start(bf16[256,2048]{1,0:T(8,128)(2,1)} %collective-permute-done.5.refs_0_), channel_id=1, source_target_pairs={{1,2},{2,1},{5,6},{6,5},{9,10},{10,9},{13,14},{14,13},{17,18},{18,... | collective-permute-start | bytes 3145736 | tf_op jit(solution)/shard_map/ppermute | solution.py:416
  219.2 33.2 %all-to-all-start.2 = ((bf16[8,72,2048]{2,1,0:T(8,128)(2,1)}), bf16[8,72,2048]{2,1,0:T(8,128)(2,1)S(1)}, u32[]{:S(2)}, u32[]{:S(2)}) async-start(bf16[8,72,2048]{2,1,0:T(8,128)(2,1)} %bitcast.72), calls=%async_computation.3 | async-start | bytes 4718592 | tf_op jit(solution)/shard_map/all_to_all | solution.py:299
  223.4 24.6 %collective-permute-start.9 = (bf16[256,2048]{1,0:T(8,128)(2,1)}, bf16[256,2048]{1,0:T(8,128)(2,1)}, u32[]{:S(2)}, u32[]{:S(2)}) collective-permute-start(bf16[256,2048]{1,0:T(8,128)(2,1)} %collective-permute-done.8.refs_0_), channel_id=1, source_target_pairs={{1,0},{2,3},{5,4},{6,7},{9,8},{10,11},{13,12},{14,15},{17,16},{18,... | collective-permute-start | bytes 3145736 | tf_op jit(solution)/shard_map/ppermute | solution.py:416
  252.3 32.8 %all-to-all-start.4 = ((bf16[8,72,2048]{2,1,0:T(8,128)(2,1)}), bf16[8,72,2048]{2,1,0:T(8,128)(2,1)}, u32[]{:S(2)}, u32[]{:S(2)}) async-start(bf16[8,72,2048]{2,1,0:T(8,128)(2,1)} %bitcast.74), calls=%async_computation.5 | async-start | bytes 4718592 | tf_op jit(solution)/shard_map/all_to_all | solution.py:299
  285.2 33.0 %all-to-all-start.5 = ((bf16[8,72,2048]{2,1,0:T(8,128)(2,1)}), bf16[8,72,2048]{2,1,0:T(8,128)(2,1)S(1)}, u32[]{:S(2)}, u32[]{:S(2)}) async-start(bf16[8,72,2048]{2,1,0:T(8,128)(2,1)} %bitcast.55), calls=%async_computation.6 | async-start | bytes 4718592 | tf_op jit(solution)/shard_map/all_to_all | solution.py:299
  319.6 36.6 %all-to-all-start.6 = ((bf16[8,72,2048]{2,1,0:T(8,128)(2,1)}), bf16[8,72,2048]{2,1,0:T(8,128)(2,1)S(1)}, u32[]{:S(2)}, u32[]{:S(2)}) async-start(bf16[8,72,2048]{2,1,0:T(8,128)(2,1)} %bitcast.28), calls=%async_computation.7 | async-start | bytes 4718592 | tf_op jit(solution)/shard_map/all_to_all | solution.py:299
  328.8 16.9 %collective-permute-start.10 = (bf16[128,2048]{1,0:T(8,128)(2,1)}, bf16[128,2048]{1,0:T(8,128)(2,1)S(1)}, u32[]{:S(2)}, u32[]{:S(2)}) collective-permute-start(bf16[128,2048]{1,0:T(8,128)(2,1)} %get-tuple-element.76), channel_id=1, source_target_pairs={{0,1},{3,2},{4,5},{7,6},{8,9},{11,10},{12,13},{15,14},{16,17},{19,... | collective-permute-start | bytes 1572872 | tf_op jit(solution)/shard_map/ppermute | solution.py:416
  330.1 26.1 %collective-permute-start.11 = (bf16[128,2048]{1,0:T(8,128)(2,1)}, bf16[128,2048]{1,0:T(8,128)(2,1)}, u32[]{:S(2)}, u32[]{:S(2)}) collective-permute-start(bf16[128,2048]{1,0:T(8,128)(2,1)} %get-tuple-element.78), channel_id=1, source_target_pairs={{0,1},{3,2},{4,5},{7,6},{8,9},{11,10},{12,13},{15,14},{16,17},{19,... | collective-permute-start | bytes 1572872 | tf_op jit(solution)/shard_map/ppermute | solution.py:416
  357.7 39.9 %all-to-all-start.7 = ((bf16[8,72,2048]{2,1,0:T(8,128)(2,1)}), bf16[8,72,2048]{2,1,0:T(8,128)(2,1)S(1)}, u32[]{:S(2)}, u32[]{:S(2)}) async-start(bf16[8,72,2048]{2,1,0:T(8,128)(2,1)} %bitcast.30), calls=%async_computation.8 | async-start | bytes 4718592 | tf_op jit(solution)/shard_map/all_to_all | solution.py:299
  366.1 29.9 %collective-permute-start.12 = (bf16[128,2048]{1,0:T(8,128)(2,1)}, bf16[128,2048]{1,0:T(8,128)(2,1)S(1)}, u32[]{:S(2)}, u32[]{:S(2)}) collective-permute-start(bf16[128,2048]{1,0:T(8,128)(2,1)} %get-tuple-element.74), channel_id=1, source_target_pairs={{0,1},{3,2},{4,5},{7,6},{8,9},{11,10},{12,13},{15,14},{16,17},{19,... | collective-permute-start | bytes 1572872 | tf_op jit(solution)/shard_map/ppermute | solution.py:416
  368.8 16.7 %collective-permute-start.15 = (bf16[128,2048]{1,0:T(8,128)(2,1)S(1)}, bf16[128,2048]{1,0:T(8,128)(2,1)S(1)}, u32[]{:S(2)}, u32[]{:S(2)}) collective-permute-start(bf16[128,2048]{1,0:T(8,128)(2,1)S(1)} %add_convert_fusion.4), channel_id=1, source_target_pairs={{1,2},{2,1},{5,6},{6,5},{9,10},{10,9},{13,14},{14,13},{17,18},{18,... | collective-permute-start | bytes 1572872 | tf_op jit(solution)/shard_map/ppermute | solution.py:416
  373.7 22.3 %collective-permute-start.14 = (bf16[128,2048]{1,0:T(8,128)(2,1)S(1)}, bf16[128,2048]{1,0:T(8,128)(2,1)S(1)}, u32[]{:S(2)}, u32[]{:S(2)}) collective-permute-start(bf16[128,2048]{1,0:T(8,128)(2,1)S(1)} %add_convert_fusion.5), channel_id=1, source_target_pairs={{1,2},{2,1},{5,6},{6,5},{9,10},{10,9},{13,14},{14,13},{17,18},{18,... | collective-permute-start | bytes 1572872 | tf_op jit(solution)/shard_map/ppermute | solution.py:416
  376.0 21.5 %collective-permute-start.13 = (bf16[128,2048]{1,0:T(8,128)(2,1)S(1)}, bf16[128,2048]{1,0:T(8,128)(2,1)}, u32[]{:S(2)}, u32[]{:S(2)}) collective-permute-start(bf16[128,2048]{1,0:T(8,128)(2,1)S(1)} %copy-done.11), channel_id=1, source_target_pairs={{0,1},{3,2},{4,5},{7,6},{8,9},{11,10},{12,13},{15,14},{16,17},{19,... | collective-permute-start | bytes 1572872 | tf_op jit(solution)/shard_map/ppermute | solution.py:416
  400.5 15.3 %collective-permute-start.16 = (bf16[128,2048]{1,0:T(8,128)(2,1)}, bf16[128,2048]{1,0:T(8,128)(2,1)}, u32[]{:S(2)}, u32[]{:S(2)}) collective-permute-start(bf16[128,2048]{1,0:T(8,128)(2,1)} %add_convert_fusion.3), channel_id=1, source_target_pairs={{1,2},{2,1},{5,6},{6,5},{9,10},{10,9},{13,14},{14,13},{17,18},{18,... | collective-permute-start | bytes 1572872 | tf_op jit(solution)/shard_map/ppermute | solution.py:416
  403.9 32.7 %all-to-all-start.8 = ((bf16[8,72,2048]{2,1,0:T(8,128)(2,1)}), bf16[8,72,2048]{2,1,0:T(8,128)(2,1)}, u32[]{:S(2)}, u32[]{:S(2)}) async-start(bf16[8,72,2048]{2,1,0:T(8,128)(2,1)} %bitcast.32), calls=%async_computation.9 | async-start | bytes 4718592 | tf_op jit(solution)/shard_map/all_to_all | solution.py:299
  417.1 14.1 %collective-permute-start.18 = (bf16[128,2048]{1,0:T(8,128)(2,1)S(1)}, bf16[128,2048]{1,0:T(8,128)(2,1)S(1)}, u32[]{:S(2)}, u32[]{:S(2)}) collective-permute-start(bf16[128,2048]{1,0:T(8,128)(2,1)S(1)} %add_convert_fusion.1), channel_id=1, source_target_pairs={{1,2},{2,1},{5,6},{6,5},{9,10},{10,9},{13,14},{14,13},{17,18},{18,... | collective-permute-start | bytes 1572872 | tf_op jit(solution)/shard_map/ppermute | solution.py:416
  426.7 14.9 %collective-permute-start.17 = (bf16[128,2048]{1,0:T(8,128)(2,1)S(1)}, bf16[128,2048]{1,0:T(8,128)(2,1)S(1)}, u32[]{:S(2)}, u32[]{:S(2)}) collective-permute-start(bf16[128,2048]{1,0:T(8,128)(2,1)S(1)} %add_convert_fusion.2), channel_id=1, source_target_pairs={{0,1},{1,0},{2,3},{3,2},{4,5},{5,4},{6,7},{7,6},{8,9},{9,8},{10,11... | collective-permute-start | bytes 1572872 | tf_op jit(solution)/shard_map/ppermute | solution.py:416
  434.0 16.0 %collective-permute-start.19 = (bf16[128,2048]{1,0:T(8,128)(2,1)}, bf16[128,2048]{1,0:T(8,128)(2,1)}, u32[]{:S(2)}, u32[]{:S(2)}) collective-permute-start(bf16[128,2048]{1,0:T(8,128)(2,1)} %add_convert_fusion), channel_id=1, source_target_pairs={{0,1},{1,0},{2,3},{3,2},{4,5},{5,4},{6,7},{7,6},{8,9},{9,8},{10,11... | collective-permute-start | bytes 1572872 | tf_op jit(solution)/shard_map/ppermute | solution.py:416
  (27 other events, 176.6 us)
Sparse Core Ops, SparseCore 0:
  59.7 77.2 reduce-scatter.1
where the time goes:
time: 463 us; the launch traced here: 460 us
  waiting for transfers between devices  184 us (40%)
  Pallas kernels  111 us (24%)
  starting transfers between devices  77.4 us (17%)
  blocking collectives  34.7 us (7%)
  other arithmetic  22.1 us (5%)
  local copies, waits for them, and re-layouts  15.6 us (3%)
  between operations  13.9 us (3%)
    ppermute x20, waiting for transfers between devices, send(): return lax.ppermute(value, 'tensor', moves)  104 us
    pallas_call x4, Pallas kernels, run_expert(): pl.pallas_call(functools.partial(expert_kernel, arrays_in=len(arrived), a...  61.3 us
    reduce_scatter x1, waiting for transfers between devices, per_device(): lax.psum_scatter(attend_and_project(slab, out_weight, heads), 'tensor', s...  52.2 us
    ppermute x20, starting transfers between devices, send(): return lax.ppermute(value, 'tensor', moves)  40.6 us
    all_to_all x8, starting transfers between devices, exchange(): lax.all_to_all(parted, 'dp', split_axis=0, concat_axis=0, tiled=True)  36.8 us
    all_to_all x1, blocking collectives, per_device(): lax.all_to_all(slabs, 'tensor', split_axis=1, concat_axis=0, tiled=True)  34.7 us
    all_to_all x8, waiting for transfers between devices, exchange(): lax.all_to_all(parted, 'dp', split_axis=0, concat_axis=0, tiled=True)  27.3 us
    pallas_call x4, Pallas kernels, combine_rows(): pl.pallas_call(combine_kernel, in_specs=[inside] * 2, out_specs=[inside]...  17.4 us
  transfers between devices with their start and end apart: 29, of which 19 were waited for; matrix products, arithmetic and copies ran while one was open for 4% of the time, Pallas kernels for 20%

commit v1 on v0

--- a/solution.py
+++ b/solution.py
@@ -409,8 +409,7 @@
         middle = [(1, 2), (2, 1)]
         outward = [(1, 0), (2, 3)]
         inward = [(0, 1), (3, 2)]
-        ends = [(0, 3), (3, 0)]
-        skips = [(1, 3), (2, 0)]
+        across = [(0, 2), (3, 1)]
 
         def send(value, moves):
             return lax.ppermute(value, "tensor", moves)
@@ -466,25 +465,24 @@
         pro3 = expert(arr3)
         ret2, pro3 = after(ret2, pro3)
         ret3 = exchange(pro3, dp_size)
-        part2 = combine(ret2, 2, arrays_out=2)
-        far2 = [send(part2[side], inward) for side in range(2)]
-        pro1, ret3, far2[0], far2[1] = after(pro1, ret3, *far2)
+        (part2,) = combine(ret2, 2)
+        outer_back2 = send(part2, across)
+        pro1, ret3, outer_back2, part2 = after(pro1, ret3, outer_back2, part2)
         ret1 = exchange(pro1, dp_size)
         part3 = combine(ret3, 3, arrays_out=2)
         far3 = [send(part3[side], inward) for side in range(2)]
-        part2[0], part2[1], _ = after(*part2, part3[0])
-        last2 = [send(short(long(part2[side]) + long(far2[side])), middle) for side in range(2)]
-        pro0, ret1, far3[0], far3[1], last2[0], last2[1] = after(pro0, ret1, *far3, *last2)
+        inner_back2 = send(part2, middle)
+        inner3 = short(long(part3[0]) + long(far3[0]))
+        pro0, ret1, inner3, inner_back2 = after(pro0, ret1, inner3, inner_back2)
         ret0 = exchange(pro0, dp_size)
-        mid3 = [send(short(long(part3[0]) + long(far3[0])), middle), None]
+        mid3 = [send(inner3, middle), None]
         mid3[0], far3[1] = after(mid3[0], far3[1])
         mid3[1] = send(short(long(part3[1]) + long(far3[1])), middle)
         part1 = combine(ret1, 1, jnp.float32, arrays_out=2)
         last1 = [send(short(part1[side] + long(mid3[side])), pairs) for side in range(2)]
         home = combine(ret0, 0, jnp.float32, arrays_out=2)
-        moe_sum = jnp.concatenate(
-            [home[side] + long(last1[side]) + long(last2[side]) for side in range(2)], axis=0
-        )
+        back1 = jnp.concatenate([home[side] + long(last1[side]) for side in range(2)], axis=0)
+        moe_sum = back1 + long(outer_back2) + long(inner_back2)
     else:
         blocks = {0: normed}
         moe_sum = 0.0

time: 463 us -> 455 us (0.983)
    convert_element_type x6 -> x4, other arithmetic: 10.4 us -> 5.97 us  [short(): return value.astype(jnp.bfloat16)]
    ppermute x20 -> x18, starting transfers between devices: 40.6 us -> 36.7 us  [send(): return lax.ppermute(value, 'tensor', moves)]
    ppermute x20 -> x18, waiting for transfers between devices: 104 us -> 105 us  [send(): return lax.ppermute(value, 'tensor', moves)]
  transfers between devices with their start and end apart: 29 -> 27, of which waited for: 19 -> 19; matrix products, arithmetic and copies ran while one was open for 4% -> 4% of each run, Pallas kernels for 20% -> 20%
where the time goes in v1:
time: 455 us; the launch traced here: 453 us
  waiting for transfers between devices  185 us (41%)
  Pallas kernels  112 us (25%)
  starting transfers between devices  75.4 us (17%)
  blocking collectives  34.7 us (8%)
  other arithmetic  18.7 us (4%)
  between operations  13.9 us (3%)
  local copies, waits for them, and re-layouts  12.9 us (3%)
    ppermute x18, waiting for transfers between devices, send(): return lax.ppermute(value, 'tensor', moves)  105 us
    pallas_call x4, Pallas kernels, run_expert(): pl.pallas_call(functools.partial(expert_kernel, arrays_in=len(arrived), a...  61.3 us
    reduce_scatter x1, waiting for transfers between devices, per_device(): lax.psum_scatter(attend_and_project(slab, out_weight, heads), 'tensor', s...  52.2 us
    all_to_all x8, starting transfers between devices, exchange(): lax.all_to_all(parted, 'dp', split_axis=0, concat_axis=0, tiled=True)  38.7 us
    ppermute x18, starting transfers between devices, send(): return lax.ppermute(value, 'tensor', moves)  36.7 us
    all_to_all x1, blocking collectives, per_device(): lax.all_to_all(slabs, 'tensor', split_axis=1, concat_axis=0, tiled=True)  34.7 us
    all_to_all x8, waiting for transfers between devices, exchange(): lax.all_to_all(parted, 'dp', split_axis=0, concat_axis=0, tiled=True)  27.7 us
    pallas_call x4, Pallas kernels, combine_rows(): pl.pallas_call(combine_kernel, in_specs=[inside] * 2, out_specs=[inside]...  17.7 us
  transfers between devices with their start and end apart: 27, of which 19 were waited for; matrix products, arithmetic and copies ran while one was open for 4% of the time, Pallas kernels for 20%

profile of v1, /device:TPU:10, one launch (start us, length us, event | category | flops | bytes accessed | tf_op | source)
XLA Modules:
  0.0 453.2 jit_solution(11593175437886689238)
XLA Ops:
  9.0 34.7 %all_to_all.55 = bf16[128,4,1280]{2,0,1:T(8,128)(2,1)S(1)} all-to-all(bf16[128,4,1280]{2,0,1:T(8,128)(2,1)S(1)} %pad_maximum_fusion), channel_id=1, replica_groups=mesh['dp'=8,'tensor'=4] {'tensor'}, dimensions={1} | all-to-all | bytes 2621440 | tf_op jit(solution)/shard_map/all_to_all | solution.py:369
  43.6 16.0 %shard_map.109 = bf16[512,4096]{1,0:T(8,128)(2,1)} custom-call(bf16[512,1280]{1,0:T(8,128)(2,1)S(1)} %bitcast.50, bf16[512,1280]{1,0:T(8,128)(2,1)S(1)} %bitcast.51, bf16[512,1280]{1,0:T(8,128)(2,1)S(1)} %bitcast.52, bf16[1024,4096]{1,0:T(8,128)(2,1)} %weight_ref.1), custom_call_target="tpu_custom_call" | custom-call | tf_op jit(solution)/shard_map/pallas_call | solution.py:83
  84.8 52.2 %reduce-scatter.2.cloned.1.call-done = bf16[128,4096]{1,0:T(8,128)(2,1)} async-done(((bf16[512,4096]{1,0:T(8,128)(2,1)}), bf16[128,4096]{1,0:T(8,128)(2,1)}) %reduce-scatter.2.cloned.1.call-update) | async-done | bytes 1048592 | tf_op jit(solution)/shard_map/reduce_scatter | solution.py:371
  152.9 21.3 %collective-permute-done.5.refs_0_ = bf16[256,2048]{1,0:T(8,128)(2,1)} collective-permute-done((bf16[256,2048]{1,0:T(8,128)(2,1)}, bf16[256,2048]{1,0:T(8,128)(2,1)}, u32[]{:S(2)}, u32[]{:S(2)}) %collective-permute-start.5) | collective-permute-done | bytes 1048608 | tf_op jit(solution)/shard_map/ppermute | solution.py:415
  180.5 4.6 %all-to-all-start.3 = ((bf16[8,72,2048]{2,1,0:T(8,128)(2,1)}), bf16[8,72,2048]{2,1,0:T(8,128)(2,1)}, u32[]{:S(2)}, u32[]{:S(2)}) async-start(bf16[8,72,2048]{2,1,0:T(8,128)(2,1)} %bitcast.68), calls=%async_computation.4 | async-start | bytes 4718592 | tf_op jit(solution)/shard_map/all_to_all | solution.py:299
  191.0 14.8 %shard_map.112 = bf16[576,2048]{1,0:T(8,128)(2,1)} custom-call(bf16[576,2048]{1,0:T(8,128)(2,1)S(1)} %bitcast.53, bf16[4096,768]{1,0:T(8,128)(2,1)} %bitcast.56, bf16[4096,768]{1,0:T(8,128)(2,1)} %bitcast.60, bf16[768,4096]{1,0:T(8,128)(2,1)} %bitcast.64), custom_call_target="tpu_custom_call" | custom-call | flops 6039797760 | bytes 40000000 | tf_op jit(solution)/shard_map/pallas_call | solution.py:196
  209.8 5.1 %collective-permute-done.8.refs_0_ = bf16[256,2048]{1,0:T(8,128)(2,1)} collective-permute-done((bf16[256,2048]{1,0:T(8,128)(2,1)}, bf16[256,2048]{1,0:T(8,128)(2,1)}, u32[]{:S(2)}, u32[]{:S(2)}) %collective-permute-start.8) | collective-permute-done | bytes 1048608 | tf_op jit(solution)/shard_map/ppermute | solution.py:415
  225.8 16.5 %shard_map.114 = bf16[576,2048]{1,0:T(8,128)(2,1)} custom-call(bf16[576,2048]{1,0:T(8,128)(2,1)} %bitcast.23.refs_0_, bf16[4096,768]{1,0:T(8,128)(2,1)} %bitcast.57, bf16[4096,768]{1,0:T(8,128)(2,1)} %bitcast.61, bf16[768,4096]{1,0:T(8,128)(2,1)} %bitcast.65), custom_call_target="tpu_custom_call" | custom-call | flops 6039797760 | bytes 40000000 | tf_op jit(solution)/shard_map/pallas_call | solution.py:196
  242.3 5.8 %collective-permute-done.9.refs_1_ = bf16[256,2048]{1,0:T(8,128)(2,1)} collective-permute-done((bf16[256,2048]{1,0:T(8,128)(2,1)}, bf16[256,2048]{1,0:T(8,128)(2,1)}, u32[]{:S(2)}, u32[]{:S(2)}) %collective-permute-start.9) | collective-permute-done | bytes 1048608 | tf_op jit(solution)/shard_map/ppermute | solution.py:415
  252.5 4.8 %all-to-all-start.4 = ((bf16[8,72,2048]{2,1,0:T(8,128)(2,1)}), bf16[8,72,2048]{2,1,0:T(8,128)(2,1)}, u32[]{:S(2)}, u32[]{:S(2)}) async-start(bf16[8,72,2048]{2,1,0:T(8,128)(2,1)} %bitcast.73), calls=%async_computation.5 | async-start | bytes 4718592 | tf_op jit(solution)/shard_map/all_to_all | solution.py:299
  257.2 13.4 %shard_map.116 = bf16[576,2048]{1,0:T(8,128)(2,1)S(1)} custom-call(bf16[576,2048]{1,0:T(8,128)(2,1)S(1)} %bitcast.54, bf16[4096,768]{1,0:T(8,128)(2,1)} %bitcast.58, bf16[4096,768]{1,0:T(8,128)(2,1)} %bitcast.62, bf16[768,4096]{1,0:T(8,128)(2,1)} %bitcast.66), custom_call_target="tpu_custom_call" | custom-call | flops 6039797760 | bytes 40000000 | tf_op jit(solution)/shard_map/pallas_call | solution.py:196
  272.1 13.2 %all-to-all-done.4 = bf16[8,72,2048]{2,1,0:T(8,128)(2,1)} async-done(((bf16[8,72,2048]{2,1,0:T(8,128)(2,1)}), bf16[8,72,2048]{2,1,0:T(8,128)(2,1)}, u32[]{:S(2)}, u32[]{:S(2)}) %all-to-all-start.4) | async-done | bytes 2359328 | tf_op jit(solution)/shard_map/all_to_all | solution.py:299
  285.3 5.0 %all-to-all-start.5 = ((bf16[8,72,2048]{2,1,0:T(8,128)(2,1)}), bf16[8,72,2048]{2,1,0:T(8,128)(2,1)S(1)}, u32[]{:S(2)}, u32[]{:S(2)}) async-start(bf16[8,72,2048]{2,1,0:T(8,128)(2,1)} %bitcast.55), calls=%async_computation.6 | async-start | bytes 4718592 | tf_op jit(solution)/shard_map/all_to_all | solution.py:299
  290.4 16.6 %shard_map.117 = bf16[576,2048]{1,0:T(8,128)(2,1)} custom-call(bf16[576,2048]{1,0:T(8,128)(2,1)} %bitcast.25.refs_0_, bf16[4096,768]{1,0:T(8,128)(2,1)} %bitcast.59, bf16[4096,768]{1,0:T(8,128)(2,1)} %bitcast.63, bf16[768,4096]{1,0:T(8,128)(2,1)} %bitcast.67), custom_call_target="tpu_custom_call" | custom-call | flops 6039797760 | bytes 40000000 | tf_op jit(solution)/shard_map/pallas_call | solution.py:196
  306.9 11.4 %all-to-all-done.5 = bf16[8,72,2048]{2,1,0:T(8,128)(2,1)S(1)} async-done(((bf16[8,72,2048]{2,1,0:T(8,128)(2,1)}), bf16[8,72,2048]{2,1,0:T(8,128)(2,1)S(1)}, u32[]{:S(2)}, u32[]{:S(2)}) %all-to-all-start.5) | async-done | bytes 2359328 | tf_op jit(solution)/shard_map/all_to_all | solution.py:299
  319.7 5.8 %all-to-all-start.6 = ((bf16[8,72,2048]{2,1,0:T(8,128)(2,1)}), bf16[8,72,2048]{2,1,0:T(8,128)(2,1)}, u32[]{:S(2)}, u32[]{:S(2)}) async-start(bf16[8,72,2048]{2,1,0:T(8,128)(2,1)} %bitcast.28), calls=%async_computation.7 | async-start | bytes 4718592 | tf_op jit(solution)/shard_map/all_to_all | solution.py:299
  331.0 27.1 %collective-permute-done.10 = bf16[256,2048]{1,0:T(8,128)(2,1)} collective-permute-done((bf16[256,2048]{1,0:T(8,128)(2,1)}, bf16[256,2048]{1,0:T(8,128)(2,1)}, u32[]{:S(2)}, u32[]{:S(2)}) %collective-permute-start.10) | collective-permute-done | bytes 1048608 | tf_op jit(solution)/shard_map/ppermute | solution.py:415
  372.6 14.3 %collective-permute-done.11 = bf16[128,2048]{1,0:T(8,128)(2,1)S(1)} collective-permute-done((bf16[128,2048]{1,0:T(8,128)(2,1)}, bf16[128,2048]{1,0:T(8,128)(2,1)S(1)}, u32[]{:S(2)}, u32[]{:S(2)}) %collective-permute-start.11) | collective-permute-done | bytes 524320 | tf_op jit(solution)/shard_map/ppermute | solution.py:415
  393.7 5.8 %all-to-all-start.8 = ((bf16[8,72,2048]{2,1,0:T(8,128)(2,1)}), bf16[8,72,2048]{2,1,0:T(8,128)(2,1)}, u32[]{:S(2)}, u32[]{:S(2)}) async-start(bf16[8,72,2048]{2,1,0:T(8,128)(2,1)} %bitcast.32), calls=%async_computation.9 | async-start | bytes 4718592 | tf_op jit(solution)/shard_map/all_to_all | solution.py:299
  399.5 7.0 %collective-permute-done.13 = bf16[128,2048]{1,0:T(8,128)(2,1)} collective-permute-done((bf16[128,2048]{1,0:T(8,128)(2,1)}, bf16[128,2048]{1,0:T(8,128)(2,1)}, u32[]{:S(2)}, u32[]{:S(2)}) %collective-permute-start.13) | collective-permute-done | bytes 524320 | tf_op jit(solution)/shard_map/ppermute | solution.py:415
  411.3 4.6 %shard_map.121 = (f32[128,2048]{1,0:T(8,128)}, f32[128,2048]{1,0:T(8,128)}) custom-call(bf16[256,576]{1,0:T(8,128)(2,1)} %bitcast.81, bf16[576,2048]{1,0:T(8,128)(2,1)} %bitcast.71), custom_call_target="tpu_custom_call" | custom-call | flops 603979776 | bytes 4000000 | tf_op jit(solution)/shard_map/pallas_call | solution.py:279
  417.5 5.4 %collective-permute-done.16 = bf16[128,2048]{1,0:T(8,128)(2,1)S(1)} collective-permute-done((bf16[128,2048]{1,0:T(8,128)(2,1)S(1)}, bf16[128,2048]{1,0:T(8,128)(2,1)S(1)}, u32[]{:S(2)}, u32[]{:S(2)}) %collective-permute-start.16) | collective-permute-done | bytes 524320 | tf_op jit(solution)/shard_map/ppermute | solution.py:415
  427.6 4.6 %shard_map.120 = (f32[128,2048]{1,0:T(8,128)}, f32[128,2048]{1,0:T(8,128)}) custom-call(bf16[256,576]{1,0:T(8,128)(2,1)} %bitcast.80, bf16[576,2048]{1,0:T(8,128)(2,1)} %bitcast.33.rows_ref), custom_call_target="tpu_custom_call" | custom-call | flops 603979776 | bytes 4000000 | tf_op jit(solution)/shard_map/pallas_call | solution.py:279
  433.8 7.8 %collective-permute-done.17 = bf16[128,2048]{1,0:T(8,128)(2,1)S(1)} collective-permute-done((bf16[128,2048]{1,0:T(8,128)(2,1)S(1)}, bf16[128,2048]{1,0:T(8,128)(2,1)S(1)}, u32[]{:S(2)}, u32[]{:S(2)}) %collective-permute-start.17) | collective-permute-done | bytes 524320 | tf_op jit(solution)/shard_map/ppermute | solution.py:415
  (126 shorter events, 121.5 us)
Async XLA Ops:
  6.5 130.5 %reduce-scatter.2.cloned.1.call-start = ((), (), s32[]{:S(2)}) async-start(), calls=%async_computation.10 | async-start | bytes 5242880 | tf_op jit(solution)/shard_map/reduce_scatter | solution.py:371
  62.2 6.0 %collective-permute-start.1 = (f32[128,16]{0,1:T(8,128)S(1)}, f32[128,16]{0,1:T(8,128)S(1)}, u32[]{:S(2)}, u32[]{:S(2)}) collective-permute-start(f32[128,16]{0,1:T(8,128)S(1)} %pad_maximum_fusion.2), channel_id=1, source_target_pairs={{1,2},{2,1},{5,6},{6,5},{9,10},{10,9},{13,14},{14,13},{17,18},{18,... | collective-permute-start | bytes 24584 | tf_op jit(solution)/shard_map/ppermute | solution.py:415
  64.8 7.4 %collective-permute-start.3 = (f32[128,16]{0,1:T(8,128)S(1)}, f32[128,16]{0,1:T(8,128)S(1)}, u32[]{:S(2)}, u32[]{:S(2)}) collective-permute-start(f32[128,16]{0,1:T(8,128)S(1)} %collective-permute-done), channel_id=1, source_target_pairs={{1,2},{2,1},{5,6},{6,5},{9,10},{10,9},{13,14},{14,13},{17,18},{18,... | collective-permute-start | bytes 24584 | tf_op jit(solution)/shard_map/ppermute | solution.py:415
  144.4 36.1 %all-to-all-start.1 = ((bf16[8,72,2048]{2,1,0:T(8,128)(2,1)}), bf16[8,72,2048]{2,1,0:T(8,128)(2,1)S(1)}, u32[]{:S(2)}, u32[]{:S(2)}) async-start(bf16[8,72,2048]{2,1,0:T(8,128)(2,1)} %bitcast.69), calls=%async_computation.2 | async-start | bytes 4718592 | tf_op jit(solution)/shard_map/all_to_all | solution.py:299
  148.6 25.5 %collective-permute-start.5 = (bf16[256,2048]{1,0:T(8,128)(2,1)}, bf16[256,2048]{1,0:T(8,128)(2,1)}, u32[]{:S(2)}, u32[]{:S(2)}) collective-permute-start(bf16[256,2048]{1,0:T(8,128)(2,1)} %pad_maximum_fusion.1.refs_0_), channel_id=1, source_target_pairs={{0,1},{1,0},{2,3},{3,2},{4,5},{5,4},{6,7},{7,6},{8,9},{9,8},{10,11... | collective-permute-start | bytes 3145736 | tf_op jit(solution)/shard_map/ppermute | solution.py:415
  149.4 27.1 %collective-permute-start.6 = (bf16[256,2048]{1,0:T(8,128)(2,1)}, bf16[256,2048]{1,0:T(8,128)(2,1)}, u32[]{:S(2)}, u32[]{:S(2)}) collective-permute-start(bf16[256,2048]{1,0:T(8,128)(2,1)} %pad_maximum_fusion.1.refs_0_), channel_id=1, source_target_pairs={{1,2},{2,1},{5,6},{6,5},{9,10},{10,9},{13,14},{14,13},{17,18},{18,... | collective-permute-start | bytes 3145736 | tf_op jit(solution)/shard_map/ppermute | solution.py:415
  180.5 38.7 %all-to-all-start.3 = ((bf16[8,72,2048]{2,1,0:T(8,128)(2,1)}), bf16[8,72,2048]{2,1,0:T(8,128)(2,1)}, u32[]{:S(2)}, u32[]{:S(2)}) async-start(bf16[8,72,2048]{2,1,0:T(8,128)(2,1)} %bitcast.68), calls=%async_computation.4 | async-start | bytes 4718592 | tf_op jit(solution)/shard_map/all_to_all | solution.py:299
  185.2 24.6 %collective-permute-start.7 = (bf16[256,2048]{1,0:T(8,128)(2,1)}, bf16[256,2048]{1,0:T(8,128)(2,1)}, u32[]{:S(2)}, u32[]{:S(2)}) collective-permute-start(bf16[256,2048]{1,0:T(8,128)(2,1)} %collective-permute-done.6.refs_0_), channel_id=1, source_target_pairs={{1,0},{2,3},{5,4},{6,7},{9,8},{10,11},{13,12},{14,15},{17,16},{18,... | collective-permute-start | bytes 3145736 | tf_op jit(solution)/shard_map/ppermute | solution.py:415
  187.5 27.4 %collective-permute-start.8 = (bf16[256,2048]{1,0:T(8,128)(2,1)}, bf16[256,2048]{1,0:T(8,128)(2,1)}, u32[]{:S(2)}, u32[]{:S(2)}) collective-permute-start(bf16[256,2048]{1,0:T(8,128)(2,1)} %collective-permute-done.5.refs_0_), channel_id=1, source_target_pairs={{1,2},{2,1},{5,6},{6,5},{9,10},{10,9},{13,14},{14,13},{17,18},{18,... | collective-permute-start | bytes 3145736 | tf_op jit(solution)/shard_map/ppermute | solution.py:415
  219.3 33.2 %all-to-all-start.2 = ((bf16[8,72,2048]{2,1,0:T(8,128)(2,1)}), bf16[8,72,2048]{2,1,0:T(8,128)(2,1)S(1)}, u32[]{:S(2)}, u32[]{:S(2)}) async-start(bf16[8,72,2048]{2,1,0:T(8,128)(2,1)} %bitcast.72), calls=%async_computation.3 | async-start | bytes 4718592 | tf_op jit(solution)/shard_map/all_to_all | solution.py:299
  223.5 24.6 %collective-permute-start.9 = (bf16[256,2048]{1,0:T(8,128)(2,1)}, bf16[256,2048]{1,0:T(8,128)(2,1)}, u32[]{:S(2)}, u32[]{:S(2)}) collective-permute-start(bf16[256,2048]{1,0:T(8,128)(2,1)} %collective-permute-done.8.refs_0_), channel_id=1, source_target_pairs={{1,0},{2,3},{5,4},{6,7},{9,8},{10,11},{13,12},{14,15},{17,16},{18,... | collective-permute-start | bytes 3145736 | tf_op jit(solution)/shard_map/ppermute | solution.py:415
  252.5 32.8 %all-to-all-start.4 = ((bf16[8,72,2048]{2,1,0:T(8,128)(2,1)}), bf16[8,72,2048]{2,1,0:T(8,128)(2,1)}, u32[]{:S(2)}, u32[]{:S(2)}) async-start(bf16[8,72,2048]{2,1,0:T(8,128)(2,1)} %bitcast.73), calls=%async_computation.5 | async-start | bytes 4718592 | tf_op jit(solution)/shard_map/all_to_all | solution.py:299
  285.3 33.0 %all-to-all-start.5 = ((bf16[8,72,2048]{2,1,0:T(8,128)(2,1)}), bf16[8,72,2048]{2,1,0:T(8,128)(2,1)S(1)}, u32[]{:S(2)}, u32[]{:S(2)}) async-start(bf16[8,72,2048]{2,1,0:T(8,128)(2,1)} %bitcast.55), calls=%async_computation.6 | async-start | bytes 4718592 | tf_op jit(solution)/shard_map/all_to_all | solution.py:299
  319.7 38.5 %all-to-all-start.6 = ((bf16[8,72,2048]{2,1,0:T(8,128)(2,1)}), bf16[8,72,2048]{2,1,0:T(8,128)(2,1)}, u32[]{:S(2)}, u32[]{:S(2)}) async-start(bf16[8,72,2048]{2,1,0:T(8,128)(2,1)} %bitcast.28), calls=%async_computation.7 | async-start | bytes 4718592 | tf_op jit(solution)/shard_map/all_to_all | solution.py:299
  329.7 28.4 %collective-permute-start.10 = (bf16[256,2048]{1,0:T(8,128)(2,1)}, bf16[256,2048]{1,0:T(8,128)(2,1)}, u32[]{:S(2)}, u32[]{:S(2)}) collective-permute-start(bf16[256,2048]{1,0:T(8,128)(2,1)} %shard_map.118), channel_id=1, source_target_pairs={{0,2},{3,1},{4,6},{7,5},{8,10},{11,9},{12,14},{15,13},{16,18},{19,... | collective-permute-start | bytes 3145736 | tf_op jit(solution)/shard_map/ppermute | solution.py:415
  358.2 32.2 %all-to-all-start.7 = ((bf16[8,72,2048]{2,1,0:T(8,128)(2,1)}), bf16[8,72,2048]{2,1,0:T(8,128)(2,1)S(1)}, u32[]{:S(2)}, u32[]{:S(2)}) async-start(bf16[8,72,2048]{2,1,0:T(8,128)(2,1)} %bitcast.30), calls=%async_computation.8 | async-start | bytes 4718592 | tf_op jit(solution)/shard_map/all_to_all | solution.py:299
  362.4 27.4 %collective-permute-start.12 = (bf16[256,2048]{1,0:T(8,128)(2,1)}, bf16[256,2048]{1,0:T(8,128)(2,1)}, u32[]{:S(2)}, u32[]{:S(2)}) collective-permute-start(bf16[256,2048]{1,0:T(8,128)(2,1)} %shard_map.118), channel_id=1, source_target_pairs={{1,2},{2,1},{5,6},{6,5},{9,10},{10,9},{13,14},{14,13},{17,18},{18,... | collective-permute-start | bytes 3145736 | tf_op jit(solution)/shard_map/ppermute | solution.py:415
  370.0 16.9 %collective-permute-start.11 = (bf16[128,2048]{1,0:T(8,128)(2,1)}, bf16[128,2048]{1,0:T(8,128)(2,1)S(1)}, u32[]{:S(2)}, u32[]{:S(2)}) collective-permute-start(bf16[128,2048]{1,0:T(8,128)(2,1)} %get-tuple-element.66), channel_id=1, source_target_pairs={{0,1},{3,2},{4,5},{7,6},{8,9},{11,10},{12,13},{15,14},{16,17},{19,... | collective-permute-start | bytes 1572872 | tf_op jit(solution)/shard_map/ppermute | solution.py:415
  371.3 28.2 %collective-permute-start.14 = (bf16[128,2048]{1,0:T(8,128)(2,1)}, bf16[128,2048]{1,0:T(8,128)(2,1)}, u32[]{:S(2)}, u32[]{:S(2)}) collective-permute-start(bf16[128,2048]{1,0:T(8,128)(2,1)} %get-tuple-element.74), channel_id=1, source_target_pairs={{0,1},{3,2},{4,5},{7,6},{8,9},{11,10},{12,13},{15,14},{16,17},{19,... | collective-permute-start | bytes 1572872 | tf_op jit(solution)/shard_map/ppermute | solution.py:415
  390.3 16.2 %collective-permute-start.13 = (bf16[128,2048]{1,0:T(8,128)(2,1)}, bf16[128,2048]{1,0:T(8,128)(2,1)}, u32[]{:S(2)}, u32[]{:S(2)}) collective-permute-start(bf16[128,2048]{1,0:T(8,128)(2,1)} %add_convert_fusion.3), channel_id=1, source_target_pairs={{1,2},{2,1},{5,6},{6,5},{9,10},{10,9},{13,14},{14,13},{17,18},{18,... | collective-permute-start | bytes 1572872 | tf_op jit(solution)/shard_map/ppermute | solution.py:415
  393.7 33.8 %all-to-all-start.8 = ((bf16[8,72,2048]{2,1,0:T(8,128)(2,1)}), bf16[8,72,2048]{2,1,0:T(8,128)(2,1)}, u32[]{:S(2)}, u32[]{:S(2)}) async-start(bf16[8,72,2048]{2,1,0:T(8,128)(2,1)} %bitcast.32), calls=%async_computation.9 | async-start | bytes 4718592 | tf_op jit(solution)/shard_map/all_to_all | solution.py:299
  407.9 15.1 %collective-permute-start.16 = (bf16[128,2048]{1,0:T(8,128)(2,1)S(1)}, bf16[128,2048]{1,0:T(8,128)(2,1)S(1)}, u32[]{:S(2)}, u32[]{:S(2)}) collective-permute-start(bf16[128,2048]{1,0:T(8,128)(2,1)S(1)} %add_convert_fusion.1), channel_id=1, source_target_pairs={{1,2},{2,1},{5,6},{6,5},{9,10},{10,9},{13,14},{14,13},{17,18},{18,... | collective-permute-start | bytes 1572872 | tf_op jit(solution)/shard_map/ppermute | solution.py:415
  417.4 14.9 %collective-permute-start.15 = (bf16[128,2048]{1,0:T(8,128)(2,1)S(1)}, bf16[128,2048]{1,0:T(8,128)(2,1)S(1)}, u32[]{:S(2)}, u32[]{:S(2)}) collective-permute-start(bf16[128,2048]{1,0:T(8,128)(2,1)S(1)} %add_convert_fusion.2), channel_id=1, source_target_pairs={{0,1},{1,0},{2,3},{3,2},{4,5},{5,4},{6,7},{7,6},{8,9},{9,8},{10,11... | collective-permute-start | bytes 1572872 | tf_op jit(solution)/shard_map/ppermute | solution.py:415
  424.9 16.7 %collective-permute-start.17 = (bf16[128,2048]{1,0:T(8,128)(2,1)S(1)}, bf16[128,2048]{1,0:T(8,128)(2,1)S(1)}, u32[]{:S(2)}, u32[]{:S(2)}) collective-permute-start(bf16[128,2048]{1,0:T(8,128)(2,1)S(1)} %add_convert_fusion), channel_id=1, source_target_pairs={{0,1},{1,0},{2,3},{3,2},{4,5},{5,4},{6,7},{7,6},{8,9},{9,8},{10,11... | collective-permute-start | bytes 1572872 | tf_op jit(solution)/shard_map/ppermute | solution.py:415
  (17 other events, 107.2 us)
Sparse Core Ops, SparseCore 0:
  59.8 77.2 reduce-scatter.1

commit v2 on v1

--- a/solution.py
+++ b/solution.py
@@ -19,7 +19,7 @@
     q_ref, k_ref, v_ref, weight_ref, o_ref, attended_ref, held_ref, sem, *, block, attend_steps
 ):
     step = pl.program_id(0)
-    scaling = 1.0 / math.sqrt(HEAD_SIZE)
+    scaling = math.log2(math.e) / math.sqrt(HEAD_SIZE)
     total, lanes = q_ref.shape
     heads = lanes // HEAD_SIZE
     fetch = pltpu.make_async_copy(weight_ref, held_ref, sem)
@@ -36,14 +36,11 @@
             seen = first + block
             mixes = []
             for head in range(heads):
-                scores = (
-                    lax.dot_general(
-                        q_ref[first:seen, head * HEAD_SIZE : (head + 1) * HEAD_SIZE],
-                        k_ref[:seen, :],
-                        (((1,), (1,)), ((), ())),
-                        preferred_element_type=jnp.float32,
-                    )
-                    * scaling
+                scores = lax.dot_general(
+                    q_ref[first:seen, head * HEAD_SIZE : (head + 1) * HEAD_SIZE],
+                    k_ref[:seen, :],
+                    (((1,), (1,)), ((), ())),
+                    preferred_element_type=jnp.float32,
                 )
                 diagonal = jnp.where(cols <= rows, scores[:, first:], -1e30)
                 if first:
@@ -51,7 +48,7 @@
                 else:
                     scores = diagonal
                 peak = jnp.max(scores, axis=-1, keepdims=True)
-                expons = jnp.exp(scores - peak)
+                expons = jnp.exp2((scores - peak) * scaling)
                 totals = jnp.sum(expons, axis=-1, keepdims=True)
                 mixed = jnp.dot(
                     expons.astype(jnp.bfloat16), v_ref[:seen, :], preferred_element_type=jnp.float32
@@ -73,11 +70,11 @@
         ).astype(jnp.bfloat16)
 
 
-def attend_and_project(slab, out_weight, heads, tile=512):
+def attend_and_project(slab, out_weight, heads, tile=1024):
     positions = slab.shape[0]
     width = out_weight.shape[1]
     out_weight = pltpu.with_memory_space_constraint(out_weight, pltpu.HBM)
-    group = 2 if heads % 2 == 0 else 1
+    group = 4 if heads % 4 == 0 else 1
     attend_steps = heads // group
     last = attend_steps - 1
     return pl.pallas_call(
@@ -433,6 +430,10 @@
         plans = list(zip(flat[::2], flat[1::2]))
 
         def dispatch(blocks, chunk):
+            if len(blocks) == 1:
+                pick = plans[chunk][0]
+                rows = jnp.dot(pick, blocks[0], preferred_element_type=jnp.float32)
+                return [rows.astype(jnp.bfloat16)]
             return gather_rows(plans[chunk][0], blocks, arrays[chunk])
 
         def combine(returned, chunk, kind=jnp.bfloat16, arrays_out=1):

time: 455 us -> 449 us (0.987)
  Pallas kernels: 112 us -> 102 us
  matrix products: 0.6 us -> 6.05 us
    pallas_call x4 -> x2, Pallas kernels: 16.8 us -> 8.75 us  [gather_rows(): pl.pallas_call(functools.partial(gather_kernel, block_count=len(blocks)),...]
    dot_general x0 -> x2, matrix products: none -> 5.45 us  [dispatch(): rows = jnp.dot(pick, blocks[0], preferred_element_type=jnp.float32)]
where the time goes in v2:
time: 449 us; the launch traced here: 448 us
  waiting for transfers between devices  186 us (41%)
  Pallas kernels  102 us (23%)
  starting transfers between devices  75.5 us (17%)
  blocking collectives  34.7 us (8%)
  other arithmetic  18.4 us (4%)
  between operations  13.9 us (3%)
  local copies, waits for them, and re-layouts  11.2 us (2%)
  matrix products  6.05 us (1%)
    ppermute x18, waiting for transfers between devices, send(): return lax.ppermute(value, 'tensor', moves)  105 us
    pallas_call x4, Pallas kernels, run_expert(): pl.pallas_call(functools.partial(expert_kernel, arrays_in=len(arrived), a...  61.3 us
    reduce_scatter x1, waiting for transfers between devices, per_device(): lax.psum_scatter(attend_and_project(slab, out_weight, heads), 'tensor', s...  53.2 us
    all_to_all x8, starting transfers between devices, exchange(): lax.all_to_all(parted, 'dp', split_axis=0, concat_axis=0, tiled=True)  38.7 us
    ppermute x18, starting transfers between devices, send(): return lax.ppermute(value, 'tensor', moves)  36.8 us
    all_to_all x1, blocking collectives, per_device(): lax.all_to_all(slabs, 'tensor', split_axis=1, concat_axis=0, tiled=True)  34.7 us
    all_to_all x8, waiting for transfers between devices, exchange(): lax.all_to_all(parted, 'dp', split_axis=0, concat_axis=0, tiled=True)  27.7 us
    pallas_call x4, Pallas kernels, combine_rows(): pl.pallas_call(combine_kernel, in_specs=[inside] * 2, out_specs=[inside]...  17.6 us
  transfers between devices with their start and end apart: 27, of which 19 were waited for; matrix products, arithmetic and copies ran while one was open for 4% of the time, Pallas kernels for 20%

profile of v2, /device:TPU:10, one launch (start us, length us, event | category | flops | bytes accessed | tf_op | source)
XLA Modules:
  0.0 447.6 jit_solution(3389937403446672315)
XLA Ops:
  9.0 34.7 %all_to_all.55 = bf16[128,4,1280]{2,0,1:T(8,128)(2,1)S(1)} all-to-all(bf16[128,4,1280]{2,0,1:T(8,128)(2,1)S(1)} %pad_maximum_fusion), channel_id=1, replica_groups=mesh['dp'=8,'tensor'=4] {'tensor'}, dimensions={1} | all-to-all | bytes 2621440 | tf_op jit(solution)/shard_map/all_to_all | solution.py:366
  43.6 13.8 %shard_map.109 = bf16[512,4096]{1,0:T(8,128)(2,1)} custom-call(bf16[512,1280]{1,0:T(8,128)(2,1)S(1)} %bitcast.56, bf16[512,1280]{1,0:T(8,128)(2,1)S(1)} %bitcast.57, bf16[512,1280]{1,0:T(8,128)(2,1)S(1)} %bitcast.58, bf16[1024,4096]{1,0:T(8,128)(2,1)} %weight_ref.1), custom_call_target="tpu_custom_call" | custom-call | tf_op jit(solution)/shard_map/pallas_call | solution.py:80
  81.7 53.2 %reduce-scatter.2.cloned.1.call-done = bf16[128,4096]{1,0:T(8,128)(2,1)} async-done(((bf16[512,4096]{1,0:T(8,128)(2,1)}), bf16[128,4096]{1,0:T(8,128)(2,1)}) %reduce-scatter.2.cloned.1.call-update) | async-done | bytes 1048592 | tf_op jit(solution)/shard_map/reduce_scatter | solution.py:368
  148.0 21.2 %collective-permute-done.5 = bf16[256,2048]{1,0:T(8,128)(2,1)S(1)} collective-permute-done((bf16[256,2048]{1,0:T(8,128)(2,1)}, bf16[256,2048]{1,0:T(8,128)(2,1)S(1)}, u32[]{:S(2)}, u32[]{:S(2)}) %collective-permute-start.5) | collective-permute-done | bytes 1048608 | tf_op jit(solution)/shard_map/ppermute | solution.py:412
  174.9 4.6 %all-to-all-start.3 = ((bf16[8,72,2048]{2,1,0:T(8,128)(2,1)}), bf16[8,72,2048]{2,1,0:T(8,128)(2,1)}, u32[]{:S(2)}, u32[]{:S(2)}) async-start(bf16[8,72,2048]{2,1,0:T(8,128)(2,1)} %bitcast.74), calls=%async_computation.4 | async-start | bytes 4718592 | tf_op jit(solution)/shard_map/all_to_all | solution.py:296
  185.5 14.9 %shard_map.110 = bf16[576,2048]{1,0:T(8,128)(2,1)} custom-call(bf16[576,2048]{1,0:T(8,128)(2,1)S(1)} %bitcast.59, bf16[4096,768]{1,0:T(8,128)(2,1)} %bitcast.62, bf16[4096,768]{1,0:T(8,128)(2,1)} %bitcast.66, bf16[768,4096]{1,0:T(8,128)(2,1)} %bitcast.70), custom_call_target="tpu_custom_call" | custom-call | flops 6039797760 | bytes 40000000 | tf_op jit(solution)/shard_map/pallas_call | solution.py:193
  204.1 5.1 %collective-permute-done.8.refs_0_ = bf16[256,2048]{1,0:T(8,128)(2,1)} collective-permute-done((bf16[256,2048]{1,0:T(8,128)(2,1)}, bf16[256,2048]{1,0:T(8,128)(2,1)}, u32[]{:S(2)}, u32[]{:S(2)}) %collective-permute-start.8) | collective-permute-done | bytes 1048608 | tf_op jit(solution)/shard_map/ppermute | solution.py:412
  220.1 16.5 %shard_map.112 = bf16[576,2048]{1,0:T(8,128)(2,1)} custom-call(bf16[576,2048]{1,0:T(8,128)(2,1)} %bitcast.23.refs_0_, bf16[4096,768]{1,0:T(8,128)(2,1)} %bitcast.63, bf16[4096,768]{1,0:T(8,128)(2,1)} %bitcast.67, bf16[768,4096]{1,0:T(8,128)(2,1)} %bitcast.71), custom_call_target="tpu_custom_call" | custom-call | flops 6039797760 | bytes 40000000 | tf_op jit(solution)/shard_map/pallas_call | solution.py:193
  236.6 5.8 %collective-permute-done.9.refs_1_ = bf16[256,2048]{1,0:T(8,128)(2,1)} collective-permute-done((bf16[256,2048]{1,0:T(8,128)(2,1)}, bf16[256,2048]{1,0:T(8,128)(2,1)}, u32[]{:S(2)}, u32[]{:S(2)}) %collective-permute-start.9) | collective-permute-done | bytes 1048608 | tf_op jit(solution)/shard_map/ppermute | solution.py:412
  246.8 4.8 %all-to-all-start.4 = ((bf16[8,72,2048]{2,1,0:T(8,128)(2,1)}), bf16[8,72,2048]{2,1,0:T(8,128)(2,1)}, u32[]{:S(2)}, u32[]{:S(2)}) async-start(bf16[8,72,2048]{2,1,0:T(8,128)(2,1)} %bitcast.79), calls=%async_computation.5 | async-start | bytes 4718592 | tf_op jit(solution)/shard_map/all_to_all | solution.py:296
  251.5 13.4 %shard_map.114 = bf16[576,2048]{1,0:T(8,128)(2,1)S(1)} custom-call(bf16[576,2048]{1,0:T(8,128)(2,1)S(1)} %bitcast.60, bf16[4096,768]{1,0:T(8,128)(2,1)} %bitcast.64, bf16[4096,768]{1,0:T(8,128)(2,1)} %bitcast.68, bf16[768,4096]{1,0:T(8,128)(2,1)} %bitcast.72), custom_call_target="tpu_custom_call" | custom-call | flops 6039797760 | bytes 40000000 | tf_op jit(solution)/shard_map/pallas_call | solution.py:193
  266.4 13.2 %all-to-all-done.4 = bf16[8,72,2048]{2,1,0:T(8,128)(2,1)} async-done(((bf16[8,72,2048]{2,1,0:T(8,128)(2,1)}), bf16[8,72,2048]{2,1,0:T(8,128)(2,1)}, u32[]{:S(2)}, u32[]{:S(2)}) %all-to-all-start.4) | async-done | bytes 2359328 | tf_op jit(solution)/shard_map/all_to_all | solution.py:296
  279.6 5.0 %all-to-all-start.5 = ((bf16[8,72,2048]{2,1,0:T(8,128)(2,1)}), bf16[8,72,2048]{2,1,0:T(8,128)(2,1)S(1)}, u32[]{:S(2)}, u32[]{:S(2)}) async-start(bf16[8,72,2048]{2,1,0:T(8,128)(2,1)} %bitcast.61), calls=%async_computation.6 | async-start | bytes 4718592 | tf_op jit(solution)/shard_map/all_to_all | solution.py:296
  284.6 16.6 %shard_map.115 = bf16[576,2048]{1,0:T(8,128)(2,1)} custom-call(bf16[576,2048]{1,0:T(8,128)(2,1)} %bitcast.25.refs_0_, bf16[4096,768]{1,0:T(8,128)(2,1)} %bitcast.65, bf16[4096,768]{1,0:T(8,128)(2,1)} %bitcast.69, bf16[768,4096]{1,0:T(8,128)(2,1)} %bitcast.73), custom_call_target="tpu_custom_call" | custom-call | flops 6039797760 | bytes 40000000 | tf_op jit(solution)/shard_map/pallas_call | solution.py:193
  301.2 11.4 %all-to-all-done.5 = bf16[8,72,2048]{2,1,0:T(8,128)(2,1)S(1)} async-done(((bf16[8,72,2048]{2,1,0:T(8,128)(2,1)}), bf16[8,72,2048]{2,1,0:T(8,128)(2,1)S(1)}, u32[]{:S(2)}, u32[]{:S(2)}) %all-to-all-start.5) | async-done | bytes 2359328 | tf_op jit(solution)/shard_map/all_to_all | solution.py:296
  314.0 5.8 %all-to-all-start.6 = ((bf16[8,72,2048]{2,1,0:T(8,128)(2,1)}), bf16[8,72,2048]{2,1,0:T(8,128)(2,1)}, u32[]{:S(2)}, u32[]{:S(2)}) async-start(bf16[8,72,2048]{2,1,0:T(8,128)(2,1)} %bitcast.28), calls=%async_computation.7 | async-start | bytes 4718592 | tf_op jit(solution)/shard_map/all_to_all | solution.py:296
  325.3 27.1 %collective-permute-done.10 = bf16[256,2048]{1,0:T(8,128)(2,1)} collective-permute-done((bf16[256,2048]{1,0:T(8,128)(2,1)}, bf16[256,2048]{1,0:T(8,128)(2,1)}, u32[]{:S(2)}, u32[]{:S(2)}) %collective-permute-start.10) | collective-permute-done | bytes 1048608 | tf_op jit(solution)/shard_map/ppermute | solution.py:412
  366.9 14.3 %collective-permute-done.11 = bf16[128,2048]{1,0:T(8,128)(2,1)S(1)} collective-permute-done((bf16[128,2048]{1,0:T(8,128)(2,1)}, bf16[128,2048]{1,0:T(8,128)(2,1)S(1)}, u32[]{:S(2)}, u32[]{:S(2)}) %collective-permute-start.11) | collective-permute-done | bytes 524320 | tf_op jit(solution)/shard_map/ppermute | solution.py:412
  388.0 5.8 %all-to-all-start.8 = ((bf16[8,72,2048]{2,1,0:T(8,128)(2,1)}), bf16[8,72,2048]{2,1,0:T(8,128)(2,1)}, u32[]{:S(2)}, u32[]{:S(2)}) async-start(bf16[8,72,2048]{2,1,0:T(8,128)(2,1)} %bitcast.32), calls=%async_computation.9 | async-start | bytes 4718592 | tf_op jit(solution)/shard_map/all_to_all | solution.py:296
  393.8 7.0 %collective-permute-done.13 = bf16[128,2048]{1,0:T(8,128)(2,1)} collective-permute-done((bf16[128,2048]{1,0:T(8,128)(2,1)}, bf16[128,2048]{1,0:T(8,128)(2,1)}, u32[]{:S(2)}, u32[]{:S(2)}) %collective-permute-start.13) | collective-permute-done | bytes 524320 | tf_op jit(solution)/shard_map/ppermute | solution.py:412
  405.6 4.6 %shard_map.119 = (f32[128,2048]{1,0:T(8,128)}, f32[128,2048]{1,0:T(8,128)}) custom-call(bf16[256,576]{1,0:T(8,128)(2,1)} %bitcast.87, bf16[576,2048]{1,0:T(8,128)(2,1)} %bitcast.77), custom_call_target="tpu_custom_call" | custom-call | flops 603979776 | bytes 4000000 | tf_op jit(solution)/shard_map/pallas_call | solution.py:276
  411.8 5.5 %collective-permute-done.16 = bf16[128,2048]{1,0:T(8,128)(2,1)S(1)} collective-permute-done((bf16[128,2048]{1,0:T(8,128)(2,1)S(1)}, bf16[128,2048]{1,0:T(8,128)(2,1)S(1)}, u32[]{:S(2)}, u32[]{:S(2)}) %collective-permute-start.16) | collective-permute-done | bytes 524320 | tf_op jit(solution)/shard_map/ppermute | solution.py:412
  421.9 4.6 %shard_map.118 = (f32[128,2048]{1,0:T(8,128)}, f32[128,2048]{1,0:T(8,128)}) custom-call(bf16[256,576]{1,0:T(8,128)(2,1)} %bitcast.86, bf16[576,2048]{1,0:T(8,128)(2,1)} %bitcast.33.rows_ref), custom_call_target="tpu_custom_call" | custom-call | flops 603979776 | bytes 4000000 | tf_op jit(solution)/shard_map/pallas_call | solution.py:276
  428.1 7.8 %collective-permute-done.17 = bf16[128,2048]{1,0:T(8,128)(2,1)S(1)} collective-permute-done((bf16[128,2048]{1,0:T(8,128)(2,1)S(1)}, bf16[128,2048]{1,0:T(8,128)(2,1)S(1)}, u32[]{:S(2)}, u32[]{:S(2)}) %collective-permute-start.17) | collective-permute-done | bytes 524320 | tf_op jit(solution)/shard_map/ppermute | solution.py:412
  (128 shorter events, 116.9 us)
Async XLA Ops:
  6.5 128.4 %reduce-scatter.2.cloned.1.call-start = ((), (), s32[]{:S(2)}) async-start(), calls=%async_computation.10 | async-start | bytes 5242880 | tf_op jit(solution)/shard_map/reduce_scatter | solution.py:368
  60.1 6.0 %collective-permute-start.1 = (f32[128,16]{0,1:T(8,128)S(1)}, f32[128,16]{0,1:T(8,128)S(1)}, u32[]{:S(2)}, u32[]{:S(2)}) collective-permute-start(f32[128,16]{0,1:T(8,128)S(1)} %pad_maximum_fusion.2), channel_id=1, source_target_pairs={{1,2},{2,1},{5,6},{6,5},{9,10},{10,9},{13,14},{14,13},{17,18},{18,... | collective-permute-start | bytes 24584 | tf_op jit(solution)/shard_map/ppermute | solution.py:412
  62.7 7.4 %collective-permute-start.3 = (f32[128,16]{0,1:T(8,128)S(1)}, f32[128,16]{0,1:T(8,128)S(1)}, u32[]{:S(2)}, u32[]{:S(2)}) collective-permute-start(f32[128,16]{0,1:T(8,128)S(1)} %collective-permute-done), channel_id=1, source_target_pairs={{1,2},{2,1},{5,6},{6,5},{9,10},{10,9},{13,14},{14,13},{17,18},{18,... | collective-permute-start | bytes 24584 | tf_op jit(solution)/shard_map/ppermute | solution.py:412
  139.5 35.4 %all-to-all-start.1 = ((bf16[8,72,2048]{2,1,0:T(8,128)(2,1)}), bf16[8,72,2048]{2,1,0:T(8,128)(2,1)S(1)}, u32[]{:S(2)}, u32[]{:S(2)}) async-start(bf16[8,72,2048]{2,1,0:T(8,128)(2,1)} %bitcast.75), calls=%async_computation.2 | async-start | bytes 4718592 | tf_op jit(solution)/shard_map/all_to_all | solution.py:296
  143.8 25.4 %collective-permute-start.5 = (bf16[256,2048]{1,0:T(8,128)(2,1)}, bf16[256,2048]{1,0:T(8,128)(2,1)S(1)}, u32[]{:S(2)}, u32[]{:S(2)}) collective-permute-start(bf16[256,2048]{1,0:T(8,128)(2,1)} %copy-done.8), channel_id=1, source_target_pairs={{0,1},{1,0},{2,3},{3,2},{4,5},{5,4},{6,7},{7,6},{8,9},{9,8},{10,11... | collective-permute-start | bytes 3145736 | tf_op jit(solution)/shard_map/ppermute | solution.py:412
  144.5 27.1 %collective-permute-start.6 = (bf16[256,2048]{1,0:T(8,128)(2,1)}, bf16[256,2048]{1,0:T(8,128)(2,1)}, u32[]{:S(2)}, u32[]{:S(2)}) collective-permute-start(bf16[256,2048]{1,0:T(8,128)(2,1)} %copy-done.8), channel_id=1, source_target_pairs={{1,2},{2,1},{5,6},{6,5},{9,10},{10,9},{13,14},{14,13},{17,18},{18,... | collective-permute-start | bytes 3145736 | tf_op jit(solution)/shard_map/ppermute | solution.py:412
  174.9 38.7 %all-to-all-start.3 = ((bf16[8,72,2048]{2,1,0:T(8,128)(2,1)}), bf16[8,72,2048]{2,1,0:T(8,128)(2,1)}, u32[]{:S(2)}, u32[]{:S(2)}) async-start(bf16[8,72,2048]{2,1,0:T(8,128)(2,1)} %bitcast.74), calls=%async_computation.4 | async-start | bytes 4718592 | tf_op jit(solution)/shard_map/all_to_all | solution.py:296
  179.5 24.6 %collective-permute-start.7 = (bf16[256,2048]{1,0:T(8,128)(2,1)}, bf16[256,2048]{1,0:T(8,128)(2,1)}, u32[]{:S(2)}, u32[]{:S(2)}) collective-permute-start(bf16[256,2048]{1,0:T(8,128)(2,1)} %collective-permute-done.6.refs_0_), channel_id=1, source_target_pairs={{1,0},{2,3},{5,4},{6,7},{9,8},{10,11},{13,12},{14,15},{17,16},{18,... | collective-permute-start | bytes 3145736 | tf_op jit(solution)/shard_map/ppermute | solution.py:412
  181.8 27.4 %collective-permute-start.8 = (bf16[256,2048]{1,0:T(8,128)(2,1)}, bf16[256,2048]{1,0:T(8,128)(2,1)}, u32[]{:S(2)}, u32[]{:S(2)}) collective-permute-start(bf16[256,2048]{1,0:T(8,128)(2,1)} %copy-done.11), channel_id=1, source_target_pairs={{1,2},{2,1},{5,6},{6,5},{9,10},{10,9},{13,14},{14,13},{17,18},{18,... | collective-permute-start | bytes 3145736 | tf_op jit(solution)/shard_map/ppermute | solution.py:412
  213.6 33.2 %all-to-all-start.2 = ((bf16[8,72,2048]{2,1,0:T(8,128)(2,1)}), bf16[8,72,2048]{2,1,0:T(8,128)(2,1)S(1)}, u32[]{:S(2)}, u32[]{:S(2)}) async-start(bf16[8,72,2048]{2,1,0:T(8,128)(2,1)} %bitcast.78), calls=%async_computation.3 | async-start | bytes 4718592 | tf_op jit(solution)/shard_map/all_to_all | solution.py:296
  217.8 24.6 %collective-permute-start.9 = (bf16[256,2048]{1,0:T(8,128)(2,1)}, bf16[256,2048]{1,0:T(8,128)(2,1)}, u32[]{:S(2)}, u32[]{:S(2)}) collective-permute-start(bf16[256,2048]{1,0:T(8,128)(2,1)} %collective-permute-done.8.refs_0_), channel_id=1, source_target_pairs={{1,0},{2,3},{5,4},{6,7},{9,8},{10,11},{13,12},{14,15},{17,16},{18,... | collective-permute-start | bytes 3145736 | tf_op jit(solution)/shard_map/ppermute | solution.py:412
  246.8 32.8 %all-to-all-start.4 = ((bf16[8,72,2048]{2,1,0:T(8,128)(2,1)}), bf16[8,72,2048]{2,1,0:T(8,128)(2,1)}, u32[]{:S(2)}, u32[]{:S(2)}) async-start(bf16[8,72,2048]{2,1,0:T(8,128)(2,1)} %bitcast.79), calls=%async_computation.5 | async-start | bytes 4718592 | tf_op jit(solution)/shard_map/all_to_all | solution.py:296
  279.6 33.0 %all-to-all-start.5 = ((bf16[8,72,2048]{2,1,0:T(8,128)(2,1)}), bf16[8,72,2048]{2,1,0:T(8,128)(2,1)S(1)}, u32[]{:S(2)}, u32[]{:S(2)}) async-start(bf16[8,72,2048]{2,1,0:T(8,128)(2,1)} %bitcast.61), calls=%async_computation.6 | async-start | bytes 4718592 | tf_op jit(solution)/shard_map/all_to_all | solution.py:296
  314.0 38.5 %all-to-all-start.6 = ((bf16[8,72,2048]{2,1,0:T(8,128)(2,1)}), bf16[8,72,2048]{2,1,0:T(8,128)(2,1)}, u32[]{:S(2)}, u32[]{:S(2)}) async-start(bf16[8,72,2048]{2,1,0:T(8,128)(2,1)} %bitcast.28), calls=%async_computation.7 | async-start | bytes 4718592 | tf_op jit(solution)/shard_map/all_to_all | solution.py:296
  324.0 28.4 %collective-permute-start.10 = (bf16[256,2048]{1,0:T(8,128)(2,1)}, bf16[256,2048]{1,0:T(8,128)(2,1)}, u32[]{:S(2)}, u32[]{:S(2)}) collective-permute-start(bf16[256,2048]{1,0:T(8,128)(2,1)} %shard_map.116), channel_id=1, source_target_pairs={{0,2},{3,1},{4,6},{7,5},{8,10},{11,9},{12,14},{15,13},{16,18},{19,... | collective-permute-start | bytes 3145736 | tf_op jit(solution)/shard_map/ppermute | solution.py:412
  352.5 32.2 %all-to-all-start.7 = ((bf16[8,72,2048]{2,1,0:T(8,128)(2,1)}), bf16[8,72,2048]{2,1,0:T(8,128)(2,1)S(1)}, u32[]{:S(2)}, u32[]{:S(2)}) async-start(bf16[8,72,2048]{2,1,0:T(8,128)(2,1)} %bitcast.30), calls=%async_computation.8 | async-start | bytes 4718592 | tf_op jit(solution)/shard_map/all_to_all | solution.py:296
  356.7 27.4 %collective-permute-start.12 = (bf16[256,2048]{1,0:T(8,128)(2,1)}, bf16[256,2048]{1,0:T(8,128)(2,1)}, u32[]{:S(2)}, u32[]{:S(2)}) collective-permute-start(bf16[256,2048]{1,0:T(8,128)(2,1)} %shard_map.116), channel_id=1, source_target_pairs={{1,2},{2,1},{5,6},{6,5},{9,10},{10,9},{13,14},{14,13},{17,18},{18,... | collective-permute-start | bytes 3145736 | tf_op jit(solution)/shard_map/ppermute | solution.py:412
  364.3 16.9 %collective-permute-start.11 = (bf16[128,2048]{1,0:T(8,128)(2,1)}, bf16[128,2048]{1,0:T(8,128)(2,1)S(1)}, u32[]{:S(2)}, u32[]{:S(2)}) collective-permute-start(bf16[128,2048]{1,0:T(8,128)(2,1)} %get-tuple-element.66), channel_id=1, source_target_pairs={{0,1},{3,2},{4,5},{7,6},{8,9},{11,10},{12,13},{15,14},{16,17},{19,... | collective-permute-start | bytes 1572872 | tf_op jit(solution)/shard_map/ppermute | solution.py:412
  365.6 28.3 %collective-permute-start.14 = (bf16[128,2048]{1,0:T(8,128)(2,1)}, bf16[128,2048]{1,0:T(8,128)(2,1)}, u32[]{:S(2)}, u32[]{:S(2)}) collective-permute-start(bf16[128,2048]{1,0:T(8,128)(2,1)} %get-tuple-element.74), channel_id=1, source_target_pairs={{0,1},{3,2},{4,5},{7,6},{8,9},{11,10},{12,13},{15,14},{16,17},{19,... | collective-permute-start | bytes 1572872 | tf_op jit(solution)/shard_map/ppermute | solution.py:412
  384.7 16.2 %collective-permute-start.13 = (bf16[128,2048]{1,0:T(8,128)(2,1)}, bf16[128,2048]{1,0:T(8,128)(2,1)}, u32[]{:S(2)}, u32[]{:S(2)}) collective-permute-start(bf16[128,2048]{1,0:T(8,128)(2,1)} %add_convert_fusion.3), channel_id=1, source_target_pairs={{1,2},{2,1},{5,6},{6,5},{9,10},{10,9},{13,14},{14,13},{17,18},{18,... | collective-permute-start | bytes 1572872 | tf_op jit(solution)/shard_map/ppermute | solution.py:412
  388.0 33.9 %all-to-all-start.8 = ((bf16[8,72,2048]{2,1,0:T(8,128)(2,1)}), bf16[8,72,2048]{2,1,0:T(8,128)(2,1)}, u32[]{:S(2)}, u32[]{:S(2)}) async-start(bf16[8,72,2048]{2,1,0:T(8,128)(2,1)} %bitcast.32), calls=%async_computation.9 | async-start | bytes 4718592 | tf_op jit(solution)/shard_map/all_to_all | solution.py:296
  402.2 15.1 %collective-permute-start.16 = (bf16[128,2048]{1,0:T(8,128)(2,1)S(1)}, bf16[128,2048]{1,0:T(8,128)(2,1)S(1)}, u32[]{:S(2)}, u32[]{:S(2)}) collective-permute-start(bf16[128,2048]{1,0:T(8,128)(2,1)S(1)} %add_convert_fusion.1), channel_id=1, source_target_pairs={{1,2},{2,1},{5,6},{6,5},{9,10},{10,9},{13,14},{14,13},{17,18},{18,... | collective-permute-start | bytes 1572872 | tf_op jit(solution)/shard_map/ppermute | solution.py:412
  411.7 14.9 %collective-permute-start.15 = (bf16[128,2048]{1,0:T(8,128)(2,1)S(1)}, bf16[128,2048]{1,0:T(8,128)(2,1)S(1)}, u32[]{:S(2)}, u32[]{:S(2)}) collective-permute-start(bf16[128,2048]{1,0:T(8,128)(2,1)S(1)} %add_convert_fusion.2), channel_id=1, source_target_pairs={{0,1},{1,0},{2,3},{3,2},{4,5},{5,4},{6,7},{7,6},{8,9},{9,8},{10,11... | collective-permute-start | bytes 1572872 | tf_op jit(solution)/shard_map/ppermute | solution.py:412
  419.2 16.7 %collective-permute-start.17 = (bf16[128,2048]{1,0:T(8,128)(2,1)S(1)}, bf16[128,2048]{1,0:T(8,128)(2,1)S(1)}, u32[]{:S(2)}, u32[]{:S(2)}) collective-permute-start(bf16[128,2048]{1,0:T(8,128)(2,1)S(1)} %add_convert_fusion), channel_id=1, source_target_pairs={{0,1},{1,0},{2,3},{3,2},{4,5},{5,4},{6,7},{7,6},{8,9},{9,8},{10,11... | collective-permute-start | bytes 1572872 | tf_op jit(solution)/shard_map/ppermute | solution.py:412
  (19 other events, 112.2 us)
Sparse Core Ops, SparseCore 0:
  57.7 77.2 reduce-scatter.1

commit v3 on v2

--- a/solution.py
+++ b/solution.py
@@ -470,8 +470,12 @@
         outer_back2 = send(part2, across)
         pro1, ret3, outer_back2, part2 = after(pro1, ret3, outer_back2, part2)
         ret1 = exchange(pro1, dp_size)
-        part3 = combine(ret3, 3, arrays_out=2)
-        far3 = [send(part3[side], inward) for side in range(2)]
+        blend3 = plans[3][1]
+        part3 = list(combine_rows(blend3[:row_count], ret3[0], jnp.bfloat16))
+        far3 = [send(part3[0], inward), None]
+        ret3[0], _ = after(ret3[0], part3[0])
+        part3 += combine_rows(blend3[row_count:], ret3[0], jnp.bfloat16)
+        far3[1] = send(part3[1], inward)
         inner_back2 = send(part2, middle)
         inner3 = short(long(part3[0]) + long(far3[0]))
         pro0, ret1, inner3, inner_back2 = after(pro0, ret1, inner3, inner_back2)

time: 449 us -> 453 us (level)
    pallas_call x4 -> x5, Pallas kernels: 17.6 us -> 20.6 us  [combine_rows(): pl.pallas_call(combine_kernel, in_specs=[inside] * 2, out_specs=[inside]...]
  transfers between devices with their start and end apart: 27 -> 27, of which waited for: 19 -> 19; matrix products, arithmetic and copies ran while one was open for 4% -> 5% of each run, Pallas kernels for 20% -> 20%
where the time goes in v3:
time: 453 us; the launch traced here: 451 us
  waiting for transfers between devices  182 us (40%)
  Pallas kernels  105 us (23%)
  starting transfers between devices  74.6 us (16%)
  blocking collectives  34.7 us (8%)
  other arithmetic  20.7 us (5%)
  local copies, waits for them, and re-layouts  15 us (3%)
  between operations  13.9 us (3%)
  matrix products  6.04 us (1%)
    ppermute x18, waiting for transfers between devices, send(): return lax.ppermute(value, 'tensor', moves)  102 us
    pallas_call x4, Pallas kernels, run_expert(): pl.pallas_call(functools.partial(expert_kernel, arrays_in=len(arrived), a...  61.3 us
    reduce_scatter x1, waiting for transfers between devices, per_device(): lax.psum_scatter(attend_and_project(slab, out_weight, heads), 'tensor', s...  53.2 us
    all_to_all x8, starting transfers between devices, exchange(): lax.all_to_all(parted, 'dp', split_axis=0, concat_axis=0, tiled=True)  37.6 us
    ppermute x18, starting transfers between devices, send(): return lax.ppermute(value, 'tensor', moves)  36.9 us
    all_to_all x1, blocking collectives, per_device(): lax.all_to_all(slabs, 'tensor', split_axis=1, concat_axis=0, tiled=True)  34.7 us
    all_to_all x8, waiting for transfers between devices, exchange(): lax.all_to_all(parted, 'dp', split_axis=0, concat_axis=0, tiled=True)  26.4 us
    pallas_call x5, Pallas kernels, combine_rows(): pl.pallas_call(combine_kernel, in_specs=[inside] * 2, out_specs=[inside]...  20.6 us
  transfers between devices with their start and end apart: 27, of which 19 were waited for; matrix products, arithmetic and copies ran while one was open for 5% of the time, Pallas kernels for 20%

profile of v3, /device:TPU:10, one launch (start us, length us, event | category | flops | bytes accessed | tf_op | source)
XLA Modules:
  0.0 451.2 jit_solution(7073008315079553098)
XLA Ops:
  9.0 34.7 %all_to_all.55 = bf16[128,4,1280]{2,0,1:T(8,128)(2,1)S(1)} all-to-all(bf16[128,4,1280]{2,0,1:T(8,128)(2,1)S(1)} %pad_maximum_fusion), channel_id=1, replica_groups=mesh['dp'=8,'tensor'=4] {'tensor'}, dimensions={1} | all-to-all | bytes 2621440 | tf_op jit(solution)/shard_map/all_to_all | solution.py:366
  43.6 13.8 %shard_map.109 = bf16[512,4096]{1,0:T(8,128)(2,1)} custom-call(bf16[512,1280]{1,0:T(8,128)(2,1)S(1)} %bitcast.56, bf16[512,1280]{1,0:T(8,128)(2,1)S(1)} %bitcast.57, bf16[512,1280]{1,0:T(8,128)(2,1)S(1)} %bitcast.58, bf16[1024,4096]{1,0:T(8,128)(2,1)} %weight_ref.1), custom_call_target="tpu_custom_call" | custom-call | tf_op jit(solution)/shard_map/pallas_call | solution.py:80
  81.7 53.2 %reduce-scatter.2.cloned.1.call-done = bf16[128,4096]{1,0:T(8,128)(2,1)} async-done(((bf16[512,4096]{1,0:T(8,128)(2,1)}), bf16[128,4096]{1,0:T(8,128)(2,1)}) %reduce-scatter.2.cloned.1.call-update) | async-done | bytes 1048592 | tf_op jit(solution)/shard_map/reduce_scatter | solution.py:368
  148.0 21.2 %collective-permute-done.5 = bf16[256,2048]{1,0:T(8,128)(2,1)S(1)} collective-permute-done((bf16[256,2048]{1,0:T(8,128)(2,1)}, bf16[256,2048]{1,0:T(8,128)(2,1)S(1)}, u32[]{:S(2)}, u32[]{:S(2)}) %collective-permute-start.5) | collective-permute-done | bytes 1048608 | tf_op jit(solution)/shard_map/ppermute | solution.py:412
  174.9 4.6 %all-to-all-start.3 = ((bf16[8,72,2048]{2,1,0:T(8,128)(2,1)}), bf16[8,72,2048]{2,1,0:T(8,128)(2,1)}, u32[]{:S(2)}, u32[]{:S(2)}) async-start(bf16[8,72,2048]{2,1,0:T(8,128)(2,1)} %bitcast.76), calls=%async_computation.4 | async-start | bytes 4718592 | tf_op jit(solution)/shard_map/all_to_all | solution.py:296
  185.5 14.9 %shard_map.110 = bf16[576,2048]{1,0:T(8,128)(2,1)} custom-call(bf16[576,2048]{1,0:T(8,128)(2,1)S(1)} %bitcast.59, bf16[4096,768]{1,0:T(8,128)(2,1)} %bitcast.62, bf16[4096,768]{1,0:T(8,128)(2,1)} %bitcast.66, bf16[768,4096]{1,0:T(8,128)(2,1)} %bitcast.70), custom_call_target="tpu_custom_call" | custom-call | flops 6039797760 | bytes 40000000 | tf_op jit(solution)/shard_map/pallas_call | solution.py:193
  204.1 5.1 %collective-permute-done.8.refs_0_ = bf16[256,2048]{1,0:T(8,128)(2,1)} collective-permute-done((bf16[256,2048]{1,0:T(8,128)(2,1)}, bf16[256,2048]{1,0:T(8,128)(2,1)}, u32[]{:S(2)}, u32[]{:S(2)}) %collective-permute-start.8) | collective-permute-done | bytes 1048608 | tf_op jit(solution)/shard_map/ppermute | solution.py:412
  220.1 16.5 %shard_map.112 = bf16[576,2048]{1,0:T(8,128)(2,1)} custom-call(bf16[576,2048]{1,0:T(8,128)(2,1)} %bitcast.23.refs_0_, bf16[4096,768]{1,0:T(8,128)(2,1)} %bitcast.63, bf16[4096,768]{1,0:T(8,128)(2,1)} %bitcast.67, bf16[768,4096]{1,0:T(8,128)(2,1)} %bitcast.71), custom_call_target="tpu_custom_call" | custom-call | flops 6039797760 | bytes 40000000 | tf_op jit(solution)/shard_map/pallas_call | solution.py:193
  236.6 5.8 %collective-permute-done.9.refs_1_ = bf16[256,2048]{1,0:T(8,128)(2,1)} collective-permute-done((bf16[256,2048]{1,0:T(8,128)(2,1)}, bf16[256,2048]{1,0:T(8,128)(2,1)}, u32[]{:S(2)}, u32[]{:S(2)}) %collective-permute-start.9) | collective-permute-done | bytes 1048608 | tf_op jit(solution)/shard_map/ppermute | solution.py:412
  246.8 4.8 %all-to-all-start.4 = ((bf16[8,72,2048]{2,1,0:T(8,128)(2,1)}), bf16[8,72,2048]{2,1,0:T(8,128)(2,1)}, u32[]{:S(2)}, u32[]{:S(2)}) async-start(bf16[8,72,2048]{2,1,0:T(8,128)(2,1)} %bitcast.81), calls=%async_computation.5 | async-start | bytes 4718592 | tf_op jit(solution)/shard_map/all_to_all | solution.py:296
  251.5 13.4 %shard_map.114 = bf16[576,2048]{1,0:T(8,128)(2,1)S(1)} custom-call(bf16[576,2048]{1,0:T(8,128)(2,1)S(1)} %bitcast.60, bf16[4096,768]{1,0:T(8,128)(2,1)} %bitcast.64, bf16[4096,768]{1,0:T(8,128)(2,1)} %bitcast.68, bf16[768,4096]{1,0:T(8,128)(2,1)} %bitcast.72), custom_call_target="tpu_custom_call" | custom-call | flops 6039797760 | bytes 40000000 | tf_op jit(solution)/shard_map/pallas_call | solution.py:193
  266.3 13.2 %all-to-all-done.4 = bf16[8,72,2048]{2,1,0:T(8,128)(2,1)} async-done(((bf16[8,72,2048]{2,1,0:T(8,128)(2,1)}), bf16[8,72,2048]{2,1,0:T(8,128)(2,1)}, u32[]{:S(2)}, u32[]{:S(2)}) %all-to-all-start.4) | async-done | bytes 2359328 | tf_op jit(solution)/shard_map/all_to_all | solution.py:296
  279.6 5.0 %all-to-all-start.5 = ((bf16[8,72,2048]{2,1,0:T(8,128)(2,1)}), bf16[8,72,2048]{2,1,0:T(8,128)(2,1)S(1)}, u32[]{:S(2)}, u32[]{:S(2)}) async-start(bf16[8,72,2048]{2,1,0:T(8,128)(2,1)} %bitcast.61), calls=%async_computation.6 | async-start | bytes 4718592 | tf_op jit(solution)/shard_map/all_to_all | solution.py:296
  284.6 16.5 %shard_map.115 = bf16[576,2048]{1,0:T(8,128)(2,1)} custom-call(bf16[576,2048]{1,0:T(8,128)(2,1)} %bitcast.25.refs_0_, bf16[4096,768]{1,0:T(8,128)(2,1)} %bitcast.65, bf16[4096,768]{1,0:T(8,128)(2,1)} %bitcast.69, bf16[768,4096]{1,0:T(8,128)(2,1)} %bitcast.73), custom_call_target="tpu_custom_call" | custom-call | flops 6039797760 | bytes 40000000 | tf_op jit(solution)/shard_map/pallas_call | solution.py:193
  301.2 11.4 %all-to-all-done.5 = bf16[8,72,2048]{2,1,0:T(8,128)(2,1)S(1)} async-done(((bf16[8,72,2048]{2,1,0:T(8,128)(2,1)}), bf16[8,72,2048]{2,1,0:T(8,128)(2,1)S(1)}, u32[]{:S(2)}, u32[]{:S(2)}) %all-to-all-start.5) | async-done | bytes 2359328 | tf_op jit(solution)/shard_map/all_to_all | solution.py:296
  314.1 5.0 %all-to-all-start.6 = ((bf16[8,72,2048]{2,1,0:T(8,128)(2,1)}), bf16[8,72,2048]{2,1,0:T(8,128)(2,1)S(1)}, u32[]{:S(2)}, u32[]{:S(2)}) async-start(bf16[8,72,2048]{2,1,0:T(8,128)(2,1)} %bitcast.28), calls=%async_computation.7 | async-start | bytes 4718592 | tf_op jit(solution)/shard_map/all_to_all | solution.py:296
  324.6 27.1 %collective-permute-done.10 = bf16[256,2048]{1,0:T(8,128)(2,1)} collective-permute-done((bf16[256,2048]{1,0:T(8,128)(2,1)}, bf16[256,2048]{1,0:T(8,128)(2,1)}, u32[]{:S(2)}, u32[]{:S(2)}) %collective-permute-start.10) | collective-permute-done | bytes 1048608 | tf_op jit(solution)/shard_map/ppermute | solution.py:412
  353.2 4.6 %all-to-all-start.7 = ((bf16[8,72,2048]{2,1,0:T(8,128)(2,1)}), bf16[8,72,2048]{2,1,0:T(8,128)(2,1)}, u32[]{:S(2)}, u32[]{:S(2)}) async-start(bf16[8,72,2048]{2,1,0:T(8,128)(2,1)} %bitcast.30), calls=%async_computation.8 | async-start | bytes 4718592 | tf_op jit(solution)/shard_map/all_to_all | solution.py:296
  373.1 10.6 %collective-permute-done.11 = bf16[128,2048]{1,0:T(8,128)(2,1)S(1)} collective-permute-done((bf16[128,2048]{1,0:T(8,128)(2,1)}, bf16[128,2048]{1,0:T(8,128)(2,1)S(1)}, u32[]{:S(2)}, u32[]{:S(2)}) %collective-permute-start.11) | collective-permute-done | bytes 524320 | tf_op jit(solution)/shard_map/ppermute | solution.py:412
  389.4 5.1 %all-to-all-start.8 = ((bf16[8,72,2048]{2,1,0:T(8,128)(2,1)}), bf16[8,72,2048]{2,1,0:T(8,128)(2,1)S(1)}, u32[]{:S(2)}, u32[]{:S(2)}) async-start(bf16[8,72,2048]{2,1,0:T(8,128)(2,1)} %bitcast.32), calls=%async_computation.9 | async-start | bytes 4718592 | tf_op jit(solution)/shard_map/all_to_all | solution.py:296
  394.4 7.6 %collective-permute-done.13 = bf16[128,2048]{1,0:T(8,128)(2,1)} collective-permute-done((bf16[128,2048]{1,0:T(8,128)(2,1)}, bf16[128,2048]{1,0:T(8,128)(2,1)}, u32[]{:S(2)}, u32[]{:S(2)}) %collective-permute-start.13) | collective-permute-done | bytes 524320 | tf_op jit(solution)/shard_map/ppermute | solution.py:412
  407.6 4.5 %shard_map.119 = (f32[128,2048]{1,0:T(8,128)}, f32[128,2048]{1,0:T(8,128)}) custom-call(bf16[256,576]{1,0:T(8,128)(2,1)} %bitcast.90, bf16[576,2048]{1,0:T(8,128)(2,1)} %bitcast.31.rows_ref), custom_call_target="tpu_custom_call" | custom-call | flops 603979776 | bytes 4000000 | tf_op jit(solution)/shard_map/pallas_call | solution.py:276
  414.5 4.9 %collective-permute-done.16 = bf16[128,2048]{1,0:T(8,128)(2,1)} collective-permute-done((bf16[128,2048]{1,0:T(8,128)(2,1)}, bf16[128,2048]{1,0:T(8,128)(2,1)}, u32[]{:S(2)}, u32[]{:S(2)}) %collective-permute-start.16) | collective-permute-done | bytes 524320 | tf_op jit(solution)/shard_map/ppermute | solution.py:412
  431.2 7.6 %collective-permute-done.17 = bf16[128,2048]{1,0:T(8,128)(2,1)} collective-permute-done((bf16[128,2048]{1,0:T(8,128)(2,1)}, bf16[128,2048]{1,0:T(8,128)(2,1)}, u32[]{:S(2)}, u32[]{:S(2)}) %collective-permute-start.17) | collective-permute-done | bytes 524320 | tf_op jit(solution)/shard_map/ppermute | solution.py:412
  (136 shorter events, 125.9 us)
Async XLA Ops:
  6.5 128.4 %reduce-scatter.2.cloned.1.call-start = ((), (), s32[]{:S(2)}) async-start(), calls=%async_computation.10 | async-start | bytes 5242880 | tf_op jit(solution)/shard_map/reduce_scatter | solution.py:368
  60.1 6.0 %collective-permute-start.1 = (f32[128,16]{0,1:T(8,128)S(1)}, f32[128,16]{0,1:T(8,128)S(1)}, u32[]{:S(2)}, u32[]{:S(2)}) collective-permute-start(f32[128,16]{0,1:T(8,128)S(1)} %pad_maximum_fusion.2), channel_id=1, source_target_pairs={{1,2},{2,1},{5,6},{6,5},{9,10},{10,9},{13,14},{14,13},{17,18},{18,... | collective-permute-start | bytes 24584 | tf_op jit(solution)/shard_map/ppermute | solution.py:412
  62.7 7.4 %collective-permute-start.3 = (f32[128,16]{0,1:T(8,128)S(1)}, f32[128,16]{0,1:T(8,128)S(1)}, u32[]{:S(2)}, u32[]{:S(2)}) collective-permute-start(f32[128,16]{0,1:T(8,128)S(1)} %collective-permute-done), channel_id=1, source_target_pairs={{1,2},{2,1},{5,6},{6,5},{9,10},{10,9},{13,14},{14,13},{17,18},{18,... | collective-permute-start | bytes 24584 | tf_op jit(solution)/shard_map/ppermute | solution.py:412
  139.5 35.3 %all-to-all-start.1 = ((bf16[8,72,2048]{2,1,0:T(8,128)(2,1)}), bf16[8,72,2048]{2,1,0:T(8,128)(2,1)S(1)}, u32[]{:S(2)}, u32[]{:S(2)}) async-start(bf16[8,72,2048]{2,1,0:T(8,128)(2,1)} %bitcast.77), calls=%async_computation.2 | async-start | bytes 4718592 | tf_op jit(solution)/shard_map/all_to_all | solution.py:296
  143.8 25.4 %collective-permute-start.5 = (bf16[256,2048]{1,0:T(8,128)(2,1)}, bf16[256,2048]{1,0:T(8,128)(2,1)S(1)}, u32[]{:S(2)}, u32[]{:S(2)}) collective-permute-start(bf16[256,2048]{1,0:T(8,128)(2,1)} %copy-done.9), channel_id=1, source_target_pairs={{0,1},{1,0},{2,3},{3,2},{4,5},{5,4},{6,7},{7,6},{8,9},{9,8},{10,11... | collective-permute-start | bytes 3145736 | tf_op jit(solution)/shard_map/ppermute | solution.py:412
  144.5 27.1 %collective-permute-start.6 = (bf16[256,2048]{1,0:T(8,128)(2,1)}, bf16[256,2048]{1,0:T(8,128)(2,1)}, u32[]{:S(2)}, u32[]{:S(2)}) collective-permute-start(bf16[256,2048]{1,0:T(8,128)(2,1)} %copy-done.9), channel_id=1, source_target_pairs={{1,2},{2,1},{5,6},{6,5},{9,10},{10,9},{13,14},{14,13},{17,18},{18,... | collective-permute-start | bytes 3145736 | tf_op jit(solution)/shard_map/ppermute | solution.py:412
  174.9 38.7 %all-to-all-start.3 = ((bf16[8,72,2048]{2,1,0:T(8,128)(2,1)}), bf16[8,72,2048]{2,1,0:T(8,128)(2,1)}, u32[]{:S(2)}, u32[]{:S(2)}) async-start(bf16[8,72,2048]{2,1,0:T(8,128)(2,1)} %bitcast.76), calls=%async_computation.4 | async-start | bytes 4718592 | tf_op jit(solution)/shard_map/all_to_all | solution.py:296
  179.5 24.6 %collective-permute-start.7 = (bf16[256,2048]{1,0:T(8,128)(2,1)}, bf16[256,2048]{1,0:T(8,128)(2,1)}, u32[]{:S(2)}, u32[]{:S(2)}) collective-permute-start(bf16[256,2048]{1,0:T(8,128)(2,1)} %collective-permute-done.6.refs_0_), channel_id=1, source_target_pairs={{1,0},{2,3},{5,4},{6,7},{9,8},{10,11},{13,12},{14,15},{17,16},{18,... | collective-permute-start | bytes 3145736 | tf_op jit(solution)/shard_map/ppermute | solution.py:412
  181.8 27.4 %collective-permute-start.8 = (bf16[256,2048]{1,0:T(8,128)(2,1)}, bf16[256,2048]{1,0:T(8,128)(2,1)}, u32[]{:S(2)}, u32[]{:S(2)}) collective-permute-start(bf16[256,2048]{1,0:T(8,128)(2,1)} %copy-done.15), channel_id=1, source_target_pairs={{1,2},{2,1},{5,6},{6,5},{9,10},{10,9},{13,14},{14,13},{17,18},{18,... | collective-permute-start | bytes 3145736 | tf_op jit(solution)/shard_map/ppermute | solution.py:412
  213.6 33.2 %all-to-all-start.2 = ((bf16[8,72,2048]{2,1,0:T(8,128)(2,1)}), bf16[8,72,2048]{2,1,0:T(8,128)(2,1)S(1)}, u32[]{:S(2)}, u32[]{:S(2)}) async-start(bf16[8,72,2048]{2,1,0:T(8,128)(2,1)} %bitcast.80), calls=%async_computation.3 | async-start | bytes 4718592 | tf_op jit(solution)/shard_map/all_to_all | solution.py:296
  217.8 24.6 %collective-permute-start.9 = (bf16[256,2048]{1,0:T(8,128)(2,1)}, bf16[256,2048]{1,0:T(8,128)(2,1)}, u32[]{:S(2)}, u32[]{:S(2)}) collective-permute-start(bf16[256,2048]{1,0:T(8,128)(2,1)} %collective-permute-done.8.refs_0_), channel_id=1, source_target_pairs={{1,0},{2,3},{5,4},{6,7},{9,8},{10,11},{13,12},{14,15},{17,16},{18,... | collective-permute-start | bytes 3145736 | tf_op jit(solution)/shard_map/ppermute | solution.py:412
  246.8 32.8 %all-to-all-start.4 = ((bf16[8,72,2048]{2,1,0:T(8,128)(2,1)}), bf16[8,72,2048]{2,1,0:T(8,128)(2,1)}, u32[]{:S(2)}, u32[]{:S(2)}) async-start(bf16[8,72,2048]{2,1,0:T(8,128)(2,1)} %bitcast.81), calls=%async_computation.5 | async-start | bytes 4718592 | tf_op jit(solution)/shard_map/all_to_all | solution.py:296
  279.6 33.0 %all-to-all-start.5 = ((bf16[8,72,2048]{2,1,0:T(8,128)(2,1)}), bf16[8,72,2048]{2,1,0:T(8,128)(2,1)S(1)}, u32[]{:S(2)}, u32[]{:S(2)}) async-start(bf16[8,72,2048]{2,1,0:T(8,128)(2,1)} %bitcast.61), calls=%async_computation.6 | async-start | bytes 4718592 | tf_op jit(solution)/shard_map/all_to_all | solution.py:296
  314.1 37.7 %all-to-all-start.6 = ((bf16[8,72,2048]{2,1,0:T(8,128)(2,1)}), bf16[8,72,2048]{2,1,0:T(8,128)(2,1)S(1)}, u32[]{:S(2)}, u32[]{:S(2)}) async-start(bf16[8,72,2048]{2,1,0:T(8,128)(2,1)} %bitcast.28), calls=%async_computation.7 | async-start | bytes 4718592 | tf_op jit(solution)/shard_map/all_to_all | solution.py:296
  323.4 28.4 %collective-permute-start.10 = (bf16[256,2048]{1,0:T(8,128)(2,1)}, bf16[256,2048]{1,0:T(8,128)(2,1)}, u32[]{:S(2)}, u32[]{:S(2)}) collective-permute-start(bf16[256,2048]{1,0:T(8,128)(2,1)} %shard_map.116), channel_id=1, source_target_pairs={{0,2},{3,1},{4,6},{7,5},{8,10},{11,9},{12,14},{15,13},{16,18},{19,... | collective-permute-start | bytes 3145736 | tf_op jit(solution)/shard_map/ppermute | solution.py:412
  353.2 32.7 %all-to-all-start.7 = ((bf16[8,72,2048]{2,1,0:T(8,128)(2,1)}), bf16[8,72,2048]{2,1,0:T(8,128)(2,1)}, u32[]{:S(2)}, u32[]{:S(2)}) async-start(bf16[8,72,2048]{2,1,0:T(8,128)(2,1)} %bitcast.30), calls=%async_computation.8 | async-start | bytes 4718592 | tf_op jit(solution)/shard_map/all_to_all | solution.py:296
  357.9 27.3 %collective-permute-start.12 = (bf16[256,2048]{1,0:T(8,128)(2,1)}, bf16[256,2048]{1,0:T(8,128)(2,1)S(1)}, u32[]{:S(2)}, u32[]{:S(2)}) collective-permute-start(bf16[256,2048]{1,0:T(8,128)(2,1)} %shard_map.116), channel_id=1, source_target_pairs={{1,2},{2,1},{5,6},{6,5},{9,10},{10,9},{13,14},{14,13},{17,18},{18,... | collective-permute-start | bytes 3145736 | tf_op jit(solution)/shard_map/ppermute | solution.py:412
  366.7 17.0 %collective-permute-start.11 = (bf16[128,2048]{1,0:T(8,128)(2,1)}, bf16[128,2048]{1,0:T(8,128)(2,1)S(1)}, u32[]{:S(2)}, u32[]{:S(2)}) collective-permute-start(bf16[128,2048]{1,0:T(8,128)(2,1)} %shard_map.117), channel_id=1, source_target_pairs={{0,1},{3,2},{4,5},{7,6},{8,9},{11,10},{12,13},{15,14},{16,17},{19,... | collective-permute-start | bytes 1572872 | tf_op jit(solution)/shard_map/ppermute | solution.py:412
  371.8 22.6 %collective-permute-start.14 = (bf16[128,2048]{1,0:T(8,128)(2,1)}, bf16[128,2048]{1,0:T(8,128)(2,1)}, u32[]{:S(2)}, u32[]{:S(2)}) collective-permute-start(bf16[128,2048]{1,0:T(8,128)(2,1)} %shard_map.120), channel_id=1, source_target_pairs={{0,1},{3,2},{4,5},{7,6},{8,9},{11,10},{12,13},{15,14},{16,17},{19,... | collective-permute-start | bytes 1572872 | tf_op jit(solution)/shard_map/ppermute | solution.py:412
  385.9 16.1 %collective-permute-start.13 = (bf16[128,2048]{1,0:T(8,128)(2,1)}, bf16[128,2048]{1,0:T(8,128)(2,1)}, u32[]{:S(2)}, u32[]{:S(2)}) collective-permute-start(bf16[128,2048]{1,0:T(8,128)(2,1)} %add_convert_fusion.3), channel_id=1, source_target_pairs={{1,2},{2,1},{5,6},{6,5},{9,10},{10,9},{13,14},{14,13},{17,18},{18,... | collective-permute-start | bytes 1572872 | tf_op jit(solution)/shard_map/ppermute | solution.py:412
  389.4 33.0 %all-to-all-start.8 = ((bf16[8,72,2048]{2,1,0:T(8,128)(2,1)}), bf16[8,72,2048]{2,1,0:T(8,128)(2,1)S(1)}, u32[]{:S(2)}, u32[]{:S(2)}) async-start(bf16[8,72,2048]{2,1,0:T(8,128)(2,1)} %bitcast.32), calls=%async_computation.9 | async-start | bytes 4718592 | tf_op jit(solution)/shard_map/all_to_all | solution.py:296
  404.2 15.3 %collective-permute-start.16 = (bf16[128,2048]{1,0:T(8,128)(2,1)}, bf16[128,2048]{1,0:T(8,128)(2,1)}, u32[]{:S(2)}, u32[]{:S(2)}) collective-permute-start(bf16[128,2048]{1,0:T(8,128)(2,1)} %add_convert_fusion.1), channel_id=1, source_target_pairs={{1,2},{2,1},{5,6},{6,5},{9,10},{10,9},{13,14},{14,13},{17,18},{18,... | collective-permute-start | bytes 1572872 | tf_op jit(solution)/shard_map/ppermute | solution.py:412
  414.5 15.2 %collective-permute-start.15 = (bf16[128,2048]{1,0:T(8,128)(2,1)}, bf16[128,2048]{1,0:T(8,128)(2,1)}, u32[]{:S(2)}, u32[]{:S(2)}) collective-permute-start(bf16[128,2048]{1,0:T(8,128)(2,1)} %add_convert_fusion.2), channel_id=1, source_target_pairs={{0,1},{1,0},{2,3},{3,2},{4,5},{5,4},{6,7},{7,6},{8,9},{9,8},{10,11... | collective-permute-start | bytes 1572872 | tf_op jit(solution)/shard_map/ppermute | solution.py:412
  421.4 17.4 %collective-permute-start.17 = (bf16[128,2048]{1,0:T(8,128)(2,1)}, bf16[128,2048]{1,0:T(8,128)(2,1)}, u32[]{:S(2)}, u32[]{:S(2)}) collective-permute-start(bf16[128,2048]{1,0:T(8,128)(2,1)} %add_convert_fusion), channel_id=1, source_target_pairs={{0,1},{1,0},{2,3},{3,2},{4,5},{5,4},{6,7},{7,6},{8,9},{9,8},{10,11... | collective-permute-start | bytes 1572872 | tf_op jit(solution)/shard_map/ppermute | solution.py:412
  (22 other events, 142.9 us)
Sparse Core Ops, SparseCore 0:
  57.7 77.2 reduce-scatter.1
